TPU v7x, 256 devices: a whole 4x4x8 slice. The times are simulated.
256 devices in a mesh: sub: 256 (over z, y, x, core).
Axes of the slice: x: 4, y: 4, z: 8, core: 2. Of those that a mesh axis runs over, the one named last changes fastest.
Arguments:
- applied_loads: float32 [294912, 128], P('sub'), may hold values from -60 to 60
- local_inverse: float32 [294912, 1152], P('sub'), may hold values from -1 to 2
- schur_block: float32 [294912, 1152], P('sub'), may hold values from -1 to 2
- coarse_modes: float32 [3072, 1152], P('sub'), may hold values from -0.1875 to 0.1875
- coarse_rows: float32 [3072, 3072], P('sub'), may hold values from -1 to 8
- mode_ids: int32 [256, 12], replicated, may hold values from 0 to 3071, as said below
- neighbours: int32 [256, 6], P('sub'), may hold values from -1 to 255, as said below
- iface_rows: int32 [256, 6, 192], P('sub'), may hold values from -1 to 1151, as said below
Outputs:
- multiplier: float32 [294912, 128], P('sub')
- displacement: float32 [294912, 128], P('sub')
Inputs may be any that keep to these rules, and one draw needn't show every extreme that they name: neighbours[s, k] is -1 or s + o_k with o = (1, -1, 4, -4, 16, -16) in a grid of 4 x 4 x 16 subdomains numbered with the first dimension fastest; t = neighbours[s, k] >= 0 gives neighbours[t, k xor 1] = s. Each list iface_rows[s, k] holds distinct rows followed by -1; it is all -1 where neighbours[s, k] = -1; the two lists of a face hold equally many rows; some list holds exactly 192 rows. mode_ids holds every mode number once.
All inputs are finite; a program needn't handle non-finite values.
Results may differ from a plain program's by a relative error of at most 0.0003.
Values sent between devices are 32-bit elements; how exact they have to be, the bound alone decides.
A program may use at most 128 MiB of HBM per device.

v0:
```python
import jax
import jax.numpy as jnp
from jax import lax
from jax.sharding import PartitionSpec as P

ITERS = 3
GRID_X = 4
GRID_Y = 4


DAMPING = 0.8
EPSILON = 1e-06
HIGHEST_PRECISION = lax.Precision.HIGHEST


def shifted(value, axis, steps):
    count = lax.axis_size(axis)
    leading, last = (max(0, -steps), min(count, count - steps))
    return lax.ppermute(value, axis, [(source, source + steps) for source in range(leading, last)])


def interface_jump(source_field, neighbours, iface_rows):
    row_lists = jnp.maximum(iface_rows[0], 0)
    usable = (iface_rows[0] >= 0) & (neighbours[0] >= 0)[:, None]
    outgoing = jnp.where(usable[:, :, None], source_field[row_lists], 0.0)
    offsets = [1, -1, GRID_X, -GRID_X, GRID_X * GRID_Y, -GRID_X * GRID_Y]
    arriving = []
    for slot_id in range(6):
        partner_slot = slot_id ^ 1
        arriving.append(shifted(outgoing[partner_slot], "sub", -offsets[slot_id]))
    incoming = jnp.stack(arriving, axis=0)
    difference = jnp.where(usable[:, :, None], outgoing - incoming, 0.0)
    return jnp.zeros_like(source_field).at[row_lists].add(difference)


def apply_block(matrix, operand):
    return jnp.dot(matrix, operand, precision=HIGHEST_PRECISION, preferred_element_type=jnp.float32)


def on_device(
    applied_loads,
    local_inverse,
    schur_block,
    coarse_modes,
    coarse_rows,
    mode_ids,
    neighbours,
    iface_rows,
):
    ordered = jnp.take(coarse_rows, mode_ids.reshape(-1), axis=1)
    modes_across = coarse_modes.T
    displacement = apply_block(local_inverse, applied_loads)
    multiplier = jnp.zeros_like(applied_loads)
    residual = interface_jump(displacement, neighbours, iface_rows)
    for sweep_id in range(ITERS):
        smoothed = apply_block(schur_block, residual)
        projected = apply_block(coarse_modes, smoothed)
        coarse = apply_block(ordered, lax.all_gather(projected, "sub", axis=0, tiled=True))
        direction = smoothed + apply_block(modes_across, coarse)
        lifted = interface_jump(direction, neighbours, iface_rows)
        response = apply_block(local_inverse, lifted)
        image_field = interface_jump(response, neighbours, iface_rows)
        numerator, denominator = lax.psum(
            (jnp.sum(residual * image_field, axis=0), jnp.sum(image_field * image_field, axis=0)),
            "sub",
        )
        step_size = DAMPING * numerator / (denominator + EPSILON)
        multiplier = multiplier + step_size * direction
        displacement = displacement - step_size * response
        residual = residual - step_size * image_field
    return (multiplier, displacement)


def solution(mesh):
    return jax.shard_map(
        on_device,
        mesh=mesh,
        in_specs=(
            P("sub", None),
            P("sub", None),
            P("sub", None),
            P("sub", None),
            P("sub", None),
            P(),
            P("sub", None),
            P("sub", None, None),
        ),
        out_specs=(P("sub", None), P("sub", None)),
        check_vma=False,
    )
```

profile of v0, /device:TPU:1, one launch (start us, length us, event | category | flops | bytes accessed | tf_op | source)
XLA Modules:
  0.0 994.6 jit_solution(11746503562408665626)
XLA Ops:
  9.5 6.3 fusion.33
  18.6 5.1 collective-permute-start
  28.1 4.7 collective-permute-start.3
  40.3 9.8 scatter_custom_fusion
  50.1 7.8 fusion.34
  61.5 12.3 %gather_fusion.1 = f32[3072,12]{1,0:T(8,128)} fusion(f32[12,3072]{0,1:T(8,128)} %copy.34, s32[3072]{0:T(1024)S(1)} %broadcast_clamp_fusion), kind=kCustom, calls=%fused_computation.1 | custom fusion | bytes 307200 | tf_op jit(solution)/shard_map/jit(_take)/gather | solution.py:50
  74.1 105.9 %all-gather.7.cloned.1.call-done = f32[256,12,128]{2,1,0:T(8,128)} async-done(((f32[1,12,128]{2,1,0:T(8,128)}), f32[256,12,128]{2,1,0:T(8,128)}) %all-gather.7.cloned.1.call-update) | async-done | bytes 1572880 | tf_op jit(solution)/shard_map/all_gather | solution.py:58
  182.6 5.0 fusion.5
  193.6 4.7 collective-permute-start.11
  212.2 10.0 %scatter_custom_fusion.1 = f32[1152,128]{1,0:T(8,128)S(1)} fusion(s32[1152]{0:T(1024)} %copy-done.18, f32[1152,128]{1,0:T(8,128)} %bitcast.255, f32[]{:T(128)} %constant.7.clone.1), kind=kCustom, calls=%fused_computation.73 | custom fusion | flops 147456 | bytes 590336 | tf_op jit(solution)/shard_map/scatter-add | solution.py:33
  222.1 6.3 convolution_bitcast_fusion.2
  235.4 11.3 %collective-permute-start.17 = (f32[192,128]{1,0:T(8,128)S(1)}, f32[192,128]{1,0:T(8,128)S(1)}, u32[]{:S(2)}, u32[]{:S(2)}) collective-permute-start(f32[192,128]{1,0:T(8,128)S(1)} %get-tuple-element.38), channel_id=1, source_target_pairs={{0,16},{1,17},{2,18},{3,19},{4,20},{5,21},{6,22},{7,23},{8,24},{9,... | collective-permute-start | bytes 294920 | tf_op jit(solution)/shard_map/ppermute | solution.py:19
  263.0 10.0 %scatter_custom_fusion.2 = f32[1152,128]{1,0:T(8,128)S(1)} fusion(s32[1152]{0:T(1024)} %copy-done.18, f32[1152,128]{1,0:T(8,128)} %bitcast.256, f32[]{:T(128)} %constant.7.clone.1), kind=kCustom, calls=%fused_computation.71 | custom fusion | flops 147456 | bytes 590336 | tf_op jit(solution)/shard_map/scatter-add | solution.py:33
  273.7 94.6 %all-reduce.2 = (f32[128]{0:T(128)}, f32[128]{0:T(128)}) all-reduce(f32[128]{0:T(128)} %get-tuple-element.7, f32[128]{0:T(128)} %get-tuple-element.6), channel_id=1, replica_groups=mesh['sub'=256] {'sub'}, use_global_device_ids=true, to_apply=%region_6.7 | all-reduce | flops 256 | bytes 2048 | tf_op jit(solution)/shard_map/psum | solution.py:63
  370.7 8.0 fusion.35
  381.2 102.0 %all-gather.9.cloned.1.call-done = f32[256,12,128]{2,1,0:T(8,128)} async-done(((f32[1,12,128]{2,1,0:T(8,128)}), f32[256,12,128]{2,1,0:T(8,128)}) %all-gather.9.cloned.1.call-update) | async-done | bytes 1572880 | tf_op jit(solution)/shard_map/all_gather | solution.py:58
  485.8 5.1 fusion.3
  498.7 4.7 collective-permute-start.23
  516.5 10.4 %scatter_custom_fusion.3 = f32[1152,128]{1,0:T(8,128)} fusion(s32[1152]{0:T(1024)} %copy-done.18, f32[1152,128]{1,0:T(8,128)S(1)} %bitcast.257, f32[]{:T(128)} %constant.7.clone.1), kind=kCustom, calls=%fused_computation.69 | custom fusion | flops 147456 | bytes 590336 | tf_op jit(solution)/shard_map/scatter-add | solution.py:33
  526.9 6.4 convolution_bitcast_fusion.1
  542.1 11.3 %collective-permute-start.29 = (f32[192,128]{1,0:T(8,128)S(1)}, f32[192,128]{1,0:T(8,128)S(1)}, u32[]{:S(2)}, u32[]{:S(2)}) collective-permute-start(f32[192,128]{1,0:T(8,128)S(1)} %get-tuple-element.26), channel_id=1, source_target_pairs={{0,16},{1,17},{2,18},{3,19},{4,20},{5,21},{6,22},{7,23},{8,24},{9,... | collective-permute-start | bytes 294920 | tf_op jit(solution)/shard_map/ppermute | solution.py:19
  569.7 10.6 %scatter_custom_fusion.4 = f32[1152,128]{1,0:T(8,128)} fusion(s32[1152]{0:T(1024)} %copy-done.18, f32[1152,128]{1,0:T(8,128)} %bitcast.258, f32[]{:T(128)} %constant.7.clone.1), kind=kCustom, calls=%fused_computation.67 | custom fusion | flops 147456 | bytes 590336 | tf_op jit(solution)/shard_map/scatter-add | solution.py:33
  582.2 94.8 %all-reduce.1 = (f32[128]{0:T(128)}, f32[128]{0:T(128)}) all-reduce(f32[128]{0:T(128)} %get-tuple-element.5, f32[128]{0:T(128)} %get-tuple-element.4), channel_id=1, replica_groups=mesh['sub'=256] {'sub'}, use_global_device_ids=true, to_apply=%region_12.13 | all-reduce | flops 256 | bytes 2048 | tf_op jit(solution)/shard_map/psum | solution.py:63
  677.7 8.0 fusion.29
  689.9 101.2 %all-gather.11.cloned.1.call-done = f32[256,12,128]{2,1,0:T(8,128)} async-done(((f32[1,12,128]{2,1,0:T(8,128)}), f32[256,12,128]{2,1,0:T(8,128)}) %all-gather.11.cloned.1.call-update) | async-done | bytes 1572880 | tf_op jit(solution)/shard_map/all_gather | solution.py:58
  793.6 5.1 fusion.7
  806.5 4.7 collective-permute-start.35
  824.2 10.4 %scatter_custom_fusion.5 = f32[1152,128]{1,0:T(8,128)} fusion(s32[1152]{0:T(1024)} %copy-done.18, f32[1152,128]{1,0:T(8,128)S(1)} %bitcast.259, f32[]{:T(128)} %constant.7.clone.1), kind=kCustom, calls=%fused_computation.65 | custom fusion | flops 147456 | bytes 590336 | tf_op jit(solution)/shard_map/scatter-add | solution.py:33
  834.7 6.4 convolution_bitcast_fusion
  849.9 11.3 %collective-permute-start.41 = (f32[192,128]{1,0:T(8,128)S(1)}, f32[192,128]{1,0:T(8,128)S(1)}, u32[]{:S(2)}, u32[]{:S(2)}) collective-permute-start(f32[192,128]{1,0:T(8,128)S(1)} %get-tuple-element.14), channel_id=1, source_target_pairs={{0,16},{1,17},{2,18},{3,19},{4,20},{5,21},{6,22},{7,23},{8,24},{9,... | collective-permute-start | bytes 294920 | tf_op jit(solution)/shard_map/ppermute | solution.py:19
  877.5 10.7 %scatter_custom_fusion.6 = f32[1152,128]{1,0:T(8,128)} fusion(s32[1152]{0:T(1024)} %copy-done.18, f32[1152,128]{1,0:T(8,128)} %bitcast.253, f32[]{:T(128)} %constant.7.clone.1), kind=kCustom, calls=%fused_computation.63 | custom fusion | flops 147456 | bytes 590336 | tf_op jit(solution)/shard_map/scatter-add | solution.py:33
  889.8 94.6 %all-reduce = (f32[128]{0:T(128)}, f32[128]{0:T(128)}) all-reduce(f32[128]{0:T(128)S(1)} %get-tuple-element.3, f32[128]{0:T(128)S(1)} %get-tuple-element.2), channel_id=1, replica_groups=mesh['sub'=256] {'sub'}, use_global_device_ids=true, to_apply=%region_18.19 | all-reduce | flops 256 | bytes 2048 | tf_op jit(solution)/shard_map/psum | solution.py:63
  (233 shorter events, 179.8 us)
Async XLA Ops:
  7.2 172.8 %all-gather.7.cloned.1.call-start = ((), (), s32[]{:S(2)}) async-start(), calls=%async_computation | async-start | bytes 2105344 | tf_op jit(solution)/shard_map/all_gather | solution.py:58
  18.6 15.5 %collective-permute-start = (f32[192,128]{1,0:T(8,128)S(1)}, f32[192,128]{1,0:T(8,128)S(1)}, u32[]{:S(2)}, u32[]{:S(2)}) collective-permute-start(f32[192,128]{1,0:T(8,128)S(1)} %get-tuple-element.55), channel_id=1, source_target_pairs={{1,0},{2,1},{3,2},{4,3},{5,4},{6,5},{7,6},{8,7},{9,8},{10,9},{11,1... | collective-permute-start | bytes 294920 | tf_op jit(solution)/shard_map/ppermute | solution.py:19
  23.7 16.3 %collective-permute-start.5 = (f32[192,128]{1,0:T(8,128)S(1)}, f32[192,128]{1,0:T(8,128)S(1)}, u32[]{:S(2)}, u32[]{:S(2)}) collective-permute-start(f32[192,128]{1,0:T(8,128)S(1)} %get-tuple-element.50), channel_id=1, source_target_pairs={{0,16},{1,17},{2,18},{3,19},{4,20},{5,21},{6,22},{7,23},{8,24},{9,... | collective-permute-start | bytes 294920 | tf_op jit(solution)/shard_map/ppermute | solution.py:19
  26.8 13.2 %collective-permute-start.4 = (f32[192,128]{1,0:T(8,128)S(1)}, f32[192,128]{1,0:T(8,128)S(1)}, u32[]{:S(2)}, u32[]{:S(2)}) collective-permute-start(f32[192,128]{1,0:T(8,128)S(1)} %get-tuple-element.51), channel_id=1, source_target_pairs={{16,0},{17,1},{18,2},{19,3},{20,4},{21,5},{22,6},{23,7},{24,8},{25... | collective-permute-start | bytes 294920 | tf_op jit(solution)/shard_map/ppermute | solution.py:19
  28.1 11.9 %collective-permute-start.3 = (f32[192,128]{1,0:T(8,128)S(1)}, f32[192,128]{1,0:T(8,128)S(1)}, u32[]{:S(2)}, u32[]{:S(2)}) collective-permute-start(f32[192,128]{1,0:T(8,128)S(1)} %get-tuple-element.52), channel_id=1, source_target_pairs={{0,4},{1,5},{2,6},{3,7},{4,8},{5,9},{6,10},{7,11},{8,12},{9,13},{1... | collective-permute-start | bytes 294920 | tf_op jit(solution)/shard_map/ppermute | solution.py:19
  59.2 424.1 %all-gather.9.cloned.1.call-start = ((), (), s32[]{:S(2)}) async-start(), calls=%async_computation.1 | async-start | bytes 2105344 | tf_op jit(solution)/shard_map/all_gather | solution.py:58
  191.4 14.0 %collective-permute-start.6 = (f32[192,128]{1,0:T(8,128)S(1)}, f32[192,128]{1,0:T(8,128)S(1)}, u32[]{:S(2)}, u32[]{:S(2)}) collective-permute-start(f32[192,128]{1,0:T(8,128)S(1)} %get-tuple-element.49), channel_id=1, source_target_pairs={{1,0},{2,1},{3,2},{4,3},{5,4},{6,5},{7,6},{8,7},{9,8},{10,9},{11,1... | collective-permute-start | bytes 294920 | tf_op jit(solution)/shard_map/ppermute | solution.py:19
  193.6 17.5 %collective-permute-start.11 = (f32[192,128]{1,0:T(8,128)S(1)}, f32[192,128]{1,0:T(8,128)S(1)}, u32[]{:S(2)}, u32[]{:S(2)}) collective-permute-start(f32[192,128]{1,0:T(8,128)S(1)} %get-tuple-element.44), channel_id=1, source_target_pairs={{0,16},{1,17},{2,18},{3,19},{4,20},{5,21},{6,22},{7,23},{8,24},{9,... | collective-permute-start | bytes 294920 | tf_op jit(solution)/shard_map/ppermute | solution.py:19
  198.3 12.8 %collective-permute-start.10 = (f32[192,128]{1,0:T(8,128)S(1)}, f32[192,128]{1,0:T(8,128)S(1)}, u32[]{:S(2)}, u32[]{:S(2)}) collective-permute-start(f32[192,128]{1,0:T(8,128)S(1)} %get-tuple-element.45), channel_id=1, source_target_pairs={{16,0},{17,1},{18,2},{19,3},{20,4},{21,5},{22,6},{23,7},{24,8},{25... | collective-permute-start | bytes 294920 | tf_op jit(solution)/shard_map/ppermute | solution.py:19
  199.6 11.5 %collective-permute-start.9 = (f32[192,128]{1,0:T(8,128)S(1)}, f32[192,128]{1,0:T(8,128)S(1)}, u32[]{:S(2)}, u32[]{:S(2)}) collective-permute-start(f32[192,128]{1,0:T(8,128)S(1)} %get-tuple-element.46), channel_id=1, source_target_pairs={{0,4},{1,5},{2,6},{3,7},{4,8},{5,9},{6,10},{7,11},{8,12},{9,13},{1... | collective-permute-start | bytes 294920 | tf_op jit(solution)/shard_map/ppermute | solution.py:19
  231.2 19.4 %collective-permute-start.12 = (f32[192,128]{1,0:T(8,128)S(1)}, f32[192,128]{1,0:T(8,128)S(1)}, u32[]{:S(2)}, u32[]{:S(2)}) collective-permute-start(f32[192,128]{1,0:T(8,128)S(1)} %get-tuple-element.43), channel_id=1, source_target_pairs={{1,0},{2,1},{3,2},{4,3},{5,4},{6,5},{7,6},{8,7},{9,8},{10,9},{11,1... | collective-permute-start | bytes 294920 | tf_op jit(solution)/shard_map/ppermute | solution.py:19
  235.4 26.6 %collective-permute-start.17 = (f32[192,128]{1,0:T(8,128)S(1)}, f32[192,128]{1,0:T(8,128)S(1)}, u32[]{:S(2)}, u32[]{:S(2)}) collective-permute-start(f32[192,128]{1,0:T(8,128)S(1)} %get-tuple-element.38), channel_id=1, source_target_pairs={{0,16},{1,17},{2,18},{3,19},{4,20},{5,21},{6,22},{7,23},{8,24},{9,... | collective-permute-start | bytes 294920 | tf_op jit(solution)/shard_map/ppermute | solution.py:19
  246.6 15.3 %collective-permute-start.16 = (f32[192,128]{1,0:T(8,128)S(1)}, f32[192,128]{1,0:T(8,128)S(1)}, u32[]{:S(2)}, u32[]{:S(2)}) collective-permute-start(f32[192,128]{1,0:T(8,128)S(1)} %get-tuple-element.39), channel_id=1, source_target_pairs={{16,0},{17,1},{18,2},{19,3},{20,4},{21,5},{22,6},{23,7},{24,8},{25... | collective-permute-start | bytes 294920 | tf_op jit(solution)/shard_map/ppermute | solution.py:19
  247.9 10.4 %collective-permute-start.15 = (f32[192,128]{1,0:T(8,128)S(1)}, f32[192,128]{1,0:T(8,128)S(1)}, u32[]{:S(2)}, u32[]{:S(2)}) collective-permute-start(f32[192,128]{1,0:T(8,128)S(1)} %get-tuple-element.40), channel_id=1, source_target_pairs={{0,4},{1,5},{2,6},{3,7},{4,8},{5,9},{6,10},{7,11},{8,12},{9,13},{1... | collective-permute-start | bytes 294920 | tf_op jit(solution)/shard_map/ppermute | solution.py:19
  249.3 9.1 collective-permute-start.14
  380.0 411.1 %all-gather.11.cloned.1.call-start = ((), (), s32[]{:S(2)}) async-start(), calls=%async_computation.2 | async-start | bytes 2105344 | tf_op jit(solution)/shard_map/all_gather | solution.py:58
  496.5 14.0 %collective-permute-start.18 = (f32[192,128]{1,0:T(8,128)S(1)}, f32[192,128]{1,0:T(8,128)S(1)}, u32[]{:S(2)}, u32[]{:S(2)}) collective-permute-start(f32[192,128]{1,0:T(8,128)S(1)} %get-tuple-element.37), channel_id=1, source_target_pairs={{1,0},{2,1},{3,2},{4,3},{5,4},{6,5},{7,6},{8,7},{9,8},{10,9},{11,1... | collective-permute-start | bytes 294920 | tf_op jit(solution)/shard_map/ppermute | solution.py:19
  498.7 17.5 %collective-permute-start.23 = (f32[192,128]{1,0:T(8,128)S(1)}, f32[192,128]{1,0:T(8,128)S(1)}, u32[]{:S(2)}, u32[]{:S(2)}) collective-permute-start(f32[192,128]{1,0:T(8,128)S(1)} %get-tuple-element.32), channel_id=1, source_target_pairs={{0,16},{1,17},{2,18},{3,19},{4,20},{5,21},{6,22},{7,23},{8,24},{9,... | collective-permute-start | bytes 294920 | tf_op jit(solution)/shard_map/ppermute | solution.py:19
  503.4 12.8 %collective-permute-start.22 = (f32[192,128]{1,0:T(8,128)S(1)}, f32[192,128]{1,0:T(8,128)S(1)}, u32[]{:S(2)}, u32[]{:S(2)}) collective-permute-start(f32[192,128]{1,0:T(8,128)S(1)} %get-tuple-element.33), channel_id=1, source_target_pairs={{16,0},{17,1},{18,2},{19,3},{20,4},{21,5},{22,6},{23,7},{24,8},{25... | collective-permute-start | bytes 294920 | tf_op jit(solution)/shard_map/ppermute | solution.py:19
  504.7 11.5 %collective-permute-start.21 = (f32[192,128]{1,0:T(8,128)S(1)}, f32[192,128]{1,0:T(8,128)S(1)}, u32[]{:S(2)}, u32[]{:S(2)}) collective-permute-start(f32[192,128]{1,0:T(8,128)S(1)} %get-tuple-element.34), channel_id=1, source_target_pairs={{0,4},{1,5},{2,6},{3,7},{4,8},{5,9},{6,10},{7,11},{8,12},{9,13},{1... | collective-permute-start | bytes 294920 | tf_op jit(solution)/shard_map/ppermute | solution.py:19
  537.9 19.4 %collective-permute-start.24 = (f32[192,128]{1,0:T(8,128)S(1)}, f32[192,128]{1,0:T(8,128)S(1)}, u32[]{:S(2)}, u32[]{:S(2)}) collective-permute-start(f32[192,128]{1,0:T(8,128)S(1)} %get-tuple-element.31), channel_id=1, source_target_pairs={{1,0},{2,1},{3,2},{4,3},{5,4},{6,5},{7,6},{8,7},{9,8},{10,9},{11,1... | collective-permute-start | bytes 294920 | tf_op jit(solution)/shard_map/ppermute | solution.py:19
  542.1 26.6 %collective-permute-start.29 = (f32[192,128]{1,0:T(8,128)S(1)}, f32[192,128]{1,0:T(8,128)S(1)}, u32[]{:S(2)}, u32[]{:S(2)}) collective-permute-start(f32[192,128]{1,0:T(8,128)S(1)} %get-tuple-element.26), channel_id=1, source_target_pairs={{0,16},{1,17},{2,18},{3,19},{4,20},{5,21},{6,22},{7,23},{8,24},{9,... | collective-permute-start | bytes 294920 | tf_op jit(solution)/shard_map/ppermute | solution.py:19
  553.4 15.3 %collective-permute-start.28 = (f32[192,128]{1,0:T(8,128)S(1)}, f32[192,128]{1,0:T(8,128)S(1)}, u32[]{:S(2)}, u32[]{:S(2)}) collective-permute-start(f32[192,128]{1,0:T(8,128)S(1)} %get-tuple-element.27), channel_id=1, source_target_pairs={{16,0},{17,1},{18,2},{19,3},{20,4},{21,5},{22,6},{23,7},{24,8},{25... | collective-permute-start | bytes 294920 | tf_op jit(solution)/shard_map/ppermute | solution.py:19
  554.7 10.4 %collective-permute-start.27 = (f32[192,128]{1,0:T(8,128)S(1)}, f32[192,128]{1,0:T(8,128)S(1)}, u32[]{:S(2)}, u32[]{:S(2)}) collective-permute-start(f32[192,128]{1,0:T(8,128)S(1)} %get-tuple-element.28), channel_id=1, source_target_pairs={{0,4},{1,5},{2,6},{3,7},{4,8},{5,9},{6,10},{7,11},{8,12},{9,13},{1... | collective-permute-start | bytes 294920 | tf_op jit(solution)/shard_map/ppermute | solution.py:19
  804.4 14.0 %collective-permute-start.30 = (f32[192,128]{1,0:T(8,128)S(1)}, f32[192,128]{1,0:T(8,128)S(1)}, u32[]{:S(2)}, u32[]{:S(2)}) collective-permute-start(f32[192,128]{1,0:T(8,128)S(1)} %get-tuple-element.25), channel_id=1, source_target_pairs={{1,0},{2,1},{3,2},{4,3},{5,4},{6,5},{7,6},{8,7},{9,8},{10,9},{11,1... | collective-permute-start | bytes 294920 | tf_op jit(solution)/shard_map/ppermute | solution.py:19
  806.5 17.4 %collective-permute-start.35 = (f32[192,128]{1,0:T(8,128)S(1)}, f32[192,128]{1,0:T(8,128)S(1)}, u32[]{:S(2)}, u32[]{:S(2)}) collective-permute-start(f32[192,128]{1,0:T(8,128)S(1)} %get-tuple-element.20), channel_id=1, source_target_pairs={{0,16},{1,17},{2,18},{3,19},{4,20},{5,21},{6,22},{7,23},{8,24},{9,... | collective-permute-start | bytes 294920 | tf_op jit(solution)/shard_map/ppermute | solution.py:19
  811.2 12.7 %collective-permute-start.34 = (f32[192,128]{1,0:T(8,128)S(1)}, f32[192,128]{1,0:T(8,128)S(1)}, u32[]{:S(2)}, u32[]{:S(2)}) collective-permute-start(f32[192,128]{1,0:T(8,128)S(1)} %get-tuple-element.21), channel_id=1, source_target_pairs={{16,0},{17,1},{18,2},{19,3},{20,4},{21,5},{22,6},{23,7},{24,8},{25... | collective-permute-start | bytes 294920 | tf_op jit(solution)/shard_map/ppermute | solution.py:19
  812.5 11.4 %collective-permute-start.33 = (f32[192,128]{1,0:T(8,128)S(1)}, f32[192,128]{1,0:T(8,128)S(1)}, u32[]{:S(2)}, u32[]{:S(2)}) collective-permute-start(f32[192,128]{1,0:T(8,128)S(1)} %get-tuple-element.22), channel_id=1, source_target_pairs={{0,4},{1,5},{2,6},{3,7},{4,8},{5,9},{6,10},{7,11},{8,12},{9,13},{1... | collective-permute-start | bytes 294920 | tf_op jit(solution)/shard_map/ppermute | solution.py:19
  845.7 19.4 %collective-permute-start.36 = (f32[192,128]{1,0:T(8,128)S(1)}, f32[192,128]{1,0:T(8,128)S(1)}, u32[]{:S(2)}, u32[]{:S(2)}) collective-permute-start(f32[192,128]{1,0:T(8,128)S(1)} %get-tuple-element.19), channel_id=1, source_target_pairs={{1,0},{2,1},{3,2},{4,3},{5,4},{6,5},{7,6},{8,7},{9,8},{10,9},{11,1... | collective-permute-start | bytes 294920 | tf_op jit(solution)/shard_map/ppermute | solution.py:19
  849.9 26.6 %collective-permute-start.41 = (f32[192,128]{1,0:T(8,128)S(1)}, f32[192,128]{1,0:T(8,128)S(1)}, u32[]{:S(2)}, u32[]{:S(2)}) collective-permute-start(f32[192,128]{1,0:T(8,128)S(1)} %get-tuple-element.14), channel_id=1, source_target_pairs={{0,16},{1,17},{2,18},{3,19},{4,20},{5,21},{6,22},{7,23},{8,24},{9,... | collective-permute-start | bytes 294920 | tf_op jit(solution)/shard_map/ppermute | solution.py:19
  861.2 15.3 %collective-permute-start.40 = (f32[192,128]{1,0:T(8,128)S(1)}, f32[192,128]{1,0:T(8,128)S(1)}, u32[]{:S(2)}, u32[]{:S(2)}) collective-permute-start(f32[192,128]{1,0:T(8,128)S(1)} %get-tuple-element.15), channel_id=1, source_target_pairs={{16,0},{17,1},{18,2},{19,3},{20,4},{21,5},{22,6},{23,7},{24,8},{25... | collective-permute-start | bytes 294920 | tf_op jit(solution)/shard_map/ppermute | solution.py:19
  862.5 10.4 %collective-permute-start.39 = (f32[192,128]{1,0:T(8,128)S(1)}, f32[192,128]{1,0:T(8,128)S(1)}, u32[]{:S(2)}, u32[]{:S(2)}) collective-permute-start(f32[192,128]{1,0:T(8,128)S(1)} %get-tuple-element.16), channel_id=1, source_target_pairs={{0,4},{1,5},{2,6},{3,7},{4,8},{5,9},{6,10},{7,11},{8,12},{9,13},{1... | collective-permute-start | bytes 294920 | tf_op jit(solution)/shard_map/ppermute | solution.py:19
  (37 other events, 800.7 us)
Sparse Core Ops, SparseCore 0:
  59.3 120.6 all-gather.6
  380.1 103.0 all-gather.8
  687.9 103.1 all-gather.10
where the time goes:
time: 1000 us; the launch traced here: 995 us
  waiting for transfers between devices  346 us (35%)
  blocking collectives  284 us (28%)
  starting transfers between devices  135 us (14%)
  other arithmetic  94.7 us (9%)
  matrix products  71.5 us (7%)
  local copies, waits for them, and re-layouts  47.4 us (5%)
  between operations  15.4 us (2%)
    all_gather x3, waiting for transfers between devices, on_device(): lax.all_gather(projected, 'sub', axis=0, tiled=True)  309 us
    psum x3, blocking collectives, on_device(): lax.psum((jnp.sum(residual * image_field, axis=0), jnp.sum(image_field *...  284 us
    ppermute x42, starting transfers between devices, shifted(): lax.ppermute(value, axis, [(source, source + steps) for source in range(l...  135 us
    scatter-add x7, other arithmetic, interface_jump(): return jnp.zeros_like(source_field).at[row_lists].add(difference)  71.9 us
    dot_general x16, matrix products, apply_block(): jnp.dot(matrix, operand, precision=HIGHEST_PRECISION, preferred_element_t...  71.5 us
    ppermute x42, waiting for transfers between devices, shifted(): lax.ppermute(value, axis, [(source, source + steps) for source in range(l...  36.9 us
  transfers between devices with their start and end apart: 45, of which 20 were waited for; matrix products, arithmetic and copies ran while one was open for 2% of the time, Pallas kernels for 0%

commit v1 on v0

v1 whole, which is shorter than its diff:
```python
import jax
import jax.numpy as jnp
from jax import lax
from jax.experimental import pallas as pl
from jax.experimental.pallas import tpu as pltpu
from jax.sharding import PartitionSpec as P

ORDER = 1152
COLS = 128
MODES_SUB = 12
IFACE = 192
SLOTS = 6
ITERS = 3
DEVICES = 256
DAMPING = 0.8
EPSILON = 1e-06
OFFSETS = (1, -1, 4, -4, 16, -16)
STRIDES = (1, 4, 16)
EXTENTS = (4, 4, 16)
GROUP = 16
BLK = 16
JUMPS = 2 + 2 * ITERS
ROUNDS = ITERS + 1
TILE = 384
F32 = jnp.float32
BF16 = jnp.bfloat16
MESH = pl.DeviceIdType.MESH
PAIRS = ((2, 3), (4, 5), (0, 1))


def dot(a, b):
    return jnp.dot(a, b, preferred_element_type=F32)


def split(value):
    high = value.astype(BF16)
    low = (value - high.astype(F32)).astype(BF16)
    return high, low


def fold(value):
    return value[:, :COLS] + value[:, COLS:]


def kernel(
    loads_hbm, inverse_hbm, schur_hbm, modes_in, rows_in, ids_in, iface_in,
    mult_hbm, disp_hbm,
    stage_k, stage_s, k_hi, k_lo, s_hi, s_lo, scatter_m, gather_m,
    out_buf, in_buf, vec, vec2, cnt, phi_t, u, w, lifted, rw, smoothed, response, gap, disp, mult, og,
    gw, m_hi, m_lo, em_hi, em_lo, ps, phi_pad, c_pad, c_send, c_recv, cb_hi, cb_lo,
    pbuf, part, rbuf, cst, coarse, mult_co,
    load_sem, out_sem, jump_send, jump_recv, c_ssem, c_rsem, p_ssem, p_rsem, q_ssem, q_rsem, n_ssem, n_rsem,
):
    me = lax.axis_index("sub")
    core = lax.rem(me, 2)
    yx = lax.rem(lax.div(me, 2), GROUP)
    zc = lax.div(me, 32) * 2 + core

    def has(slot):
        axis = slot // 2
        place = lax.rem(lax.div(me, STRIDES[axis]), EXTENTS[axis])
        return place < EXTENTS[axis] - 1 if slot % 2 == 0 else place > 0

    def along_z(index):
        return lax.div(index, 2) * 32 + yx * 2 + lax.rem(index, 2)

    def along_plane(index):
        return lax.div(me, 32) * 32 + index * 2 + core

    copies_k, copies_s = [], []
    load_copy = pltpu.make_async_copy(loads_hbm, disp, load_sem.at[6])
    load_copy.start()
    for i in range(3):
        part_rows = pl.ds(i * TILE, TILE)
        copy = pltpu.make_async_copy(inverse_hbm.at[part_rows], stage_k.at[part_rows], load_sem.at[i])
        copy.start()
        copies_k.append(copy)
    for i in range(3):
        part_rows = pl.ds(i * TILE, TILE)
        copy = pltpu.make_async_copy(schur_hbm.at[part_rows], stage_s.at[part_rows], load_sem.at[3 + i])
        copy.start()
        copies_s.append(copy)

    barrier = pltpu.get_barrier_semaphore()

    def greet(step, carry):
        pl.semaphore_signal(barrier, inc=1, device_id=(along_z(lax.rem(zc + step, GROUP)),), device_id_type=MESH)
        pl.semaphore_signal(barrier, inc=1, device_id=(along_plane(lax.rem(yx + step, GROUP)),), device_id_type=MESH)
        return carry

    lax.fori_loop(1, GROUP, greet, 0)
    present = jnp.int32(0)
    for slot in range(SLOTS):
        there = has(slot)
        present = present + jnp.where(there, 1, 0)

        @pl.when(there)
        def _(slot=slot):
            pl.semaphore_signal(barrier, inc=1, device_id=(me + OFFSETS[slot],), device_id_type=MESH)

    row_of = iface_in[...]

    @pl.loop(0, 9)
    def _(i):
        rows = pl.ds(pl.multiple_of(i * 128, 128), 128)
        ids = lax.broadcasted_iota(jnp.int32, (128, ORDER), 0) + i * 128
        scatter_m[rows, :] = jnp.where(ids == row_of, 1.0, 0.0).astype(BF16)
        across = jnp.broadcast_to(iface_in[:, rows], (128, 128)).T
        for c in range(9):
            lanes = lax.broadcasted_iota(jnp.int32, (128, 128), 1) + c * 128
            gather_m[rows, c * 128:(c + 1) * 128] = jnp.where(lanes == across, 1.0, 0.0).astype(BF16)

    phi_pad[...] = jnp.zeros_like(phi_pad)
    phi_pad[0:MODES_SUB, :] = modes_in[...]
    for c in range(9):
        piece = phi_pad[:, c * 128:(c + 1) * 128]
        phi_t[c * 128:(c + 1) * 128, :] = jnp.concatenate([piece] * 8, axis=0).T

    c_pad[...] = jnp.zeros_like(c_pad)
    c_pad[0:MODES_SUB, :] = rows_in[...]
    for half in range(2):
        @pl.loop(0, GROUP)
        def _(target, half=half):
            ids = ids_in[target, :, half * 128:(half + 1) * 128]
            ids = jnp.broadcast_to(ids, (8, 128))
            tile_id = lax.shift_right_arithmetic(ids, 7)
            lane_id = lax.bitwise_and(ids, 127)
            lane = lax.broadcasted_iota(jnp.int32, (8, 128), 1)
            sub = lax.broadcasted_iota(jnp.int32, (8, 128), 0)
            mode = lax.bitwise_and(lane, 15)
            for octet in range(2):
                total = jnp.zeros((8, 128), F32)
                for src in range(24):
                    piece = c_pad[octet * 8:(octet + 1) * 8, src * 128:(src + 1) * 128]
                    picked = jnp.take_along_axis(piece, lane_id, axis=1)
                    total = jnp.where(tile_id == src, picked, total)
                if octet == 1:
                    keep = (mode == sub + 8) & (mode >= 12) & (mode < 14)
                    total = jnp.where(keep, 1.0, total)
                c_send[target, octet * 8:(octet + 1) * 8, half * 128:(half + 1) * 128] = total

    ones = jnp.ones((ORDER, COLS), BF16)
    cnt[...] = dot(scatter_m[...], ones)

    for slot in range(SLOTS):
        @pl.when(jnp.logical_not(has(slot)))
        def _(slot=slot):
            for j in range(JUMPS):
                in_buf[j, slot * IFACE:(slot + 1) * IFACE, :] = jnp.zeros((IFACE, COLS), F32)
            for n in range(ITERS):
                cst[n, slot + 1] = jnp.zeros((BLK, COLS), F32)
    for n in range(ITERS):
        cst[n, 7] = jnp.zeros((BLK, COLS), F32)

    def load_vec(ref_to, value):
        high, low = split(value)
        ref_to[:, :COLS] = high
        ref_to[:, COLS:] = low

    def product(high_ref, low_ref, vec_ref, into):
        @pl.loop(0, ORDER // TILE)
        def _(i):
            rows = pl.ds(pl.multiple_of(i * TILE, TILE), TILE)
            total = dot(high_ref[rows, :], vec_ref[...]) + dot(low_ref[rows, :], vec_ref[...])
            into[rows, :] = fold(total)

    def scattered(jump, own):
        load_vec(vec, in_buf[jump])

        def body(i, carry):
            rows = pl.ds(pl.multiple_of(i * TILE, TILE), TILE)
            own[rows, :] = own[rows, :] - fold(dot(scatter_m[rows, :], vec[...]))
            return carry

        lax.fori_loop(0, ORDER // TILE, body, 0)

    def jump_copy(jump, slot):
        return pltpu.make_async_remote_copy(
            src_ref=out_buf.at[jump, pl.ds(slot * IFACE, IFACE)],
            dst_ref=in_buf.at[jump, pl.ds((slot ^ 1) * IFACE, IFACE)],
            send_sem=jump_send.at[jump, slot],
            recv_sem=jump_recv.at[jump, slot ^ 1],
            device_id=(me + OFFSETS[slot],),
            device_id_type=MESH,
        )

    def jump_arrival(jump, slot):
        return pltpu.make_async_remote_copy(
            src_ref=out_buf.at[jump, pl.ds(slot * IFACE, IFACE)],
            dst_ref=in_buf.at[jump, pl.ds(slot * IFACE, IFACE)],
            send_sem=jump_send.at[jump, slot],
            recv_sem=jump_recv.at[jump, slot],
            device_id=(me + OFFSETS[slot],),
            device_id_type=MESH,
        )

    def send_slot(jump, slot):
        @pl.when(has(slot))
        def _():
            jump_copy(jump, slot).start()

    def await_jump(jump):
        for slot in range(SLOTS):
            @pl.when(has(slot))
            def _(slot=slot):
                jump_arrival(jump, slot).wait_recv()

    def gather_send(jump, vec_ref):
        for first, second in PAIRS:
            rows = slice(first * IFACE, (second + 1) * IFACE)
            out_buf[jump, rows, :] = fold(dot(gather_m[rows, :], vec_ref[...]))
            send_slot(jump, first)
            send_slot(jump, second)

    load_copy.wait()
    load_vec(vec, disp[...])
    for i in range(3):
        copies_k[i].wait()
        rows = slice(i * TILE, (i + 1) * TILE)
        high, low = split(stage_k[rows, :])
        k_hi[rows, :] = high
        k_lo[rows, :] = low
    product(k_hi, k_lo, vec, disp)
    load_vec(vec, disp[...])
    pl.semaphore_wait(barrier, 2 * (GROUP - 1) + present)
    gather_send(1, vec)

    load_vec(vec2, phi_t[...])
    lane_block = lax.div(lax.broadcasted_iota(jnp.int32, (IFACE, COLS), 1), BLK)
    for slot in range(SLOTS):
        rows = slice(slot * IFACE, (slot + 1) * IFACE)
        value = fold(dot(gather_m[rows, :], vec2[...]))
        out_buf[0, rows, :] = jnp.where(lane_block == 1 + (slot ^ 1), value, 0.0)
        send_slot(0, slot)

    def send_coarse(step, carry):
        peer = lax.rem(yx + step, GROUP)
        pltpu.make_async_remote_copy(
            src_ref=c_send.at[peer], dst_ref=c_recv.at[yx], send_sem=c_ssem, recv_sem=c_rsem,
            device_id=(along_plane(peer),), device_id_type=MESH,
        ).start()
        return carry

    lax.fori_loop(1, GROUP, send_coarse, 0)
    c_recv[pl.ds(yx, 1)] = c_send[pl.ds(yx, 1)]

    for i in range(3):
        copies_s[i].wait()
        rows = slice(i * TILE, (i + 1) * TILE)
        high, low = split(stage_s[rows, :])
        s_hi[rows, :] = high
        s_lo[rows, :] = low
    high, low = split(phi_pad[...])
    both = jnp.concatenate([high, low], axis=0)
    for c in range(3):
        lanes = slice(c * TILE, (c + 1) * TILE)
        total = dot(both, s_hi[:, lanes]) + dot(both, s_lo[:, lanes])
        high, low = split(total[:BLK] + total[BLK:])
        ps[0:BLK, lanes] = high
        ps[BLK:, lanes] = low

    await_jump(0)
    lane = lax.broadcasted_iota(jnp.int32, (ORDER, COLS), 1)
    rw[...] = jnp.where(lane < BLK, phi_t[...] * cnt[...], 0.0)
    scattered(0, rw)
    load_vec(vec2, rw[...])
    product(k_hi, k_lo, vec2, rw)
    high, low = split(rw[...])
    m_hi[...] = high
    m_lo[...] = low
    vec2[:, :COLS] = high
    vec2[:, COLS:] = low
    for i in range(3):
        rows = slice(i * TILE, (i + 1) * TILE)
        total = dot(gather_m[rows, :], vec2[...])
        em_hi[rows, :] = total[:, :COLS].astype(BF16)
        em_lo[rows, :] = total[:, COLS:].astype(BF16)

    pltpu.make_async_remote_copy(
        src_ref=c_send.at[pl.ds(0, GROUP - 1)], dst_ref=c_recv.at[pl.ds(0, GROUP - 1)], send_sem=c_ssem, recv_sem=c_rsem,
        device_id=(along_plane(lax.rem(yx + 1, GROUP)),), device_id_type=MESH,
    ).wait()
    high, low = split(c_recv[...].reshape(GROUP * BLK, GROUP * BLK))
    cb_hi[...] = high
    cb_lo[...] = low

    smoothed[...] = jnp.zeros_like(smoothed)
    response[...] = jnp.zeros_like(response)
    gap[...] = jnp.zeros_like(gap)
    mult[...] = jnp.zeros_like(mult)
    coarse[...] = jnp.zeros_like(coarse)
    mult_co[...] = jnp.zeros_like(mult_co)

    await_jump(1)
    u[...] = cnt[...] * disp[...]
    scattered(1, u)

    def first_round(n):
        load_vec(vec, u[...])
        total = dot(ps[...], vec[...])
        total = fold(total[:BLK] + total[BLK:])
        upper = jnp.sum(gap[...] * u[...], axis=0, keepdims=True)
        lower = jnp.sum(u[...] * u[...], axis=0, keepdims=True)
        row = lax.broadcasted_iota(jnp.int32, (BLK, COLS), 0)
        upper = jnp.where(n == 0, 0.0, upper)
        lower = jnp.where(n == 0, 0.0, lower)
        total = jnp.where(row == 12, upper, jnp.where(row == 13, lower, total))
        pbuf[n, pl.ds(zc, 1)] = total[None]

        def send(step, carry):
            pltpu.make_async_remote_copy(
                src_ref=pbuf.at[n, zc], dst_ref=pbuf.at[n, zc], send_sem=p_ssem.at[n], recv_sem=p_rsem.at[n],
                device_id=(along_z(lax.rem(zc + step, GROUP)),), device_id_type=MESH,
            ).start()
            return carry

        lax.fori_loop(1, GROUP, send, 0)

    def whole(src, dst, ssem, rsem):
        return pltpu.make_async_remote_copy(
            src_ref=src, dst_ref=dst, send_sem=ssem, recv_sem=rsem,
            device_id=(along_z(lax.rem(zc + 1, GROUP)),), device_id_type=MESH,
        )

    def p_whole(n):
        return whole(pbuf.at[n, pl.ds(0, GROUP - 1)], pbuf.at[n, pl.ds(0, GROUP - 1)], p_ssem.at[n], p_rsem.at[n])

    def q_whole(n):
        return whole(part.at[n, pl.ds(0, GROUP - 1)], rbuf.at[n, pl.ds(0, GROUP - 1)], q_ssem.at[n], q_rsem.at[n])

    def second_round(n):
        p_whole(n).wait_recv()
        high, low = split(pbuf[n].reshape(GROUP * BLK, COLS))
        both = jnp.concatenate([high, low], axis=1)
        total = fold(dot(cb_hi[...], both) + dot(cb_lo[...], both))
        part[n] = total.reshape(GROUP, BLK, COLS)

        def send(step, carry):
            peer = lax.rem(yx + step, GROUP)
            pltpu.make_async_remote_copy(
                src_ref=part.at[n, peer], dst_ref=rbuf.at[n, yx], send_sem=q_ssem.at[n], recv_sem=q_rsem.at[n],
                device_id=(along_plane(peer),), device_id_type=MESH,
            ).start()
            return carry

        lax.fori_loop(1, GROUP, send, 0)
        rbuf[n, pl.ds(yx, 1)] = part[n, pl.ds(yx, 1)]

    def sums(n):
        q_whole(n).wait_recv()
        total = jnp.sum(rbuf[n], axis=0)
        return total, DAMPING * total[12:13] / (total[13:14] + EPSILON)

    def near_copy(n, slot, arriving):
        return pltpu.make_async_remote_copy(
            src_ref=cst.at[n, 0],
            dst_ref=cst.at[n, 1 + (slot if arriving else slot ^ 1)],
            send_sem=n_ssem.at[n, slot],
            recv_sem=n_rsem.at[n, slot if arriving else slot ^ 1],
            device_id=(me + OFFSETS[slot],),
            device_id_type=MESH,
        )

    def sweep(n, carry):
        first_round(n)
        product(s_hi, s_lo, vec, w)
        load_vec(vec2, w[...])
        gather_send(2 + 2 * n, vec2)
        second_round(n)
        await_jump(2 + 2 * n)
        lifted[...] = cnt[...] * w[...]
        scattered(2 + 2 * n, lifted)
        total, step = sums(n)
        step = jnp.where(n == 0, -1.0, step)
        total = jnp.where(lax.broadcasted_iota(jnp.int32, (BLK, COLS), 0) < MODES_SUB, total, 0.0)
        cst[n, 0] = total
        for slot in range(SLOTS):
            @pl.when(has(slot))
            def _(slot=slot):
                near_copy(n, slot, False).start()
        load_vec(vec, lifted[...])
        product(k_hi, k_lo, vec, rw)
        load_vec(vec, rw[...])
        for i in range(3):
            rows = slice(i * TILE, (i + 1) * TILE)
            gw[rows, :] = fold(dot(gather_m[rows, :], vec[...]))
        for slot in range(SLOTS):
            @pl.when(has(slot))
            def _(slot=slot):
                near_copy(n, slot, True).wait_recv()
        high, low = split(cst[n].reshape(8 * BLK, COLS))
        near = jnp.concatenate([high, low], axis=1)
        jump = 3 + 2 * n
        for first, second in PAIRS:
            rows = slice(first * IFACE, (second + 1) * IFACE)
            change = gw[rows, :] + fold(dot(em_hi[rows, :], near) + dot(em_lo[rows, :], near))
            og[rows, :] = og[rows, :] - step * change
            out_buf[jump, rows, :] = og[rows, :]
            send_slot(jump, first)
            send_slot(jump, second)
        update(step)
        gap[...] = gap[...] - step * u[...]
        smoothed[...] = smoothed[...] - step * w[...]
        coarse[...] = coarse[...] - step * total

        def body(i, inner):
            rows = pl.ds(pl.multiple_of(i * TILE, TILE), TILE)
            change = rw[rows, :] + fold(dot(m_hi[rows, :], near) + dot(m_lo[rows, :], near))
            response[rows, :] = response[rows, :] - step * change
            return inner

        lax.fori_loop(0, ORDER // TILE, body, 0)
        u[...] = cnt[...] * response[...]
        await_jump(jump)
        scattered(jump, u)
        return carry

    def update(step):
        mult[...] = mult[...] + step * smoothed[...]
        mult_co[...] = mult_co[...] + step * coarse[...]
        disp[...] = disp[...] - step * response[...]

    og[...] = jnp.zeros_like(og)
    lax.fori_loop(0, ITERS, sweep, 0)

    first_round(ITERS)
    high, low = split(jnp.where(lane < BLK, phi_t[...], 0.0))
    m_hi[...] = high
    m_lo[...] = low
    second_round(ITERS)
    total, step = sums(ITERS)
    update(step)
    out_d = pltpu.make_async_copy(disp, disp_hbm, out_sem.at[0])
    out_d.start()
    padded = jnp.concatenate([mult_co[...], jnp.zeros((COLS - BLK, COLS), F32)], axis=0)
    high, low = split(padded)
    both = jnp.concatenate([high, low], axis=1)
    mult[...] = mult[...] + fold(dot(m_hi[...], both) + dot(m_lo[...], both))
    out_m = pltpu.make_async_copy(mult, mult_hbm, out_sem.at[1])
    out_m.start()

    for slot in range(SLOTS):
        @pl.when(has(slot))
        def _(slot=slot):
            def jump_left(jump, carry):
                jump_copy(jump, slot).wait_send()
                return carry

            lax.fori_loop(0, JUMPS, jump_left, 0)

            def near_left(n, carry):
                near_copy(n, slot, False).wait_send()
                return carry

            lax.fori_loop(0, ITERS, near_left, 0)

    def rounds_left(n, carry):
        p_whole(n).wait_send()
        q_whole(n).wait_send()
        return carry

    lax.fori_loop(0, ROUNDS, rounds_left, 0)
    out_d.wait()
    out_m.wait()


def on_device(
    applied_loads,
    local_inverse,
    schur_block,
    coarse_modes,
    coarse_rows,
    mode_ids,
    neighbours,
    iface_rows,
):
    ids = mode_ids.reshape(DEVICES // 32, GROUP, 2, MODES_SUB).transpose(1, 0, 2, 3)
    ids = jnp.pad(ids, ((0, 0), (0, 0), (0, 0), (0, BLK - MODES_SUB)), constant_values=-1)
    ids = ids.reshape(GROUP, 1, GROUP * BLK)
    field = pltpu.VMEM((ORDER, COLS), F32)
    square = pltpu.VMEM((ORDER, ORDER), BF16)
    vector = pltpu.VMEM((ORDER, 2 * COLS), BF16)
    slim = pltpu.VMEM((ORDER, COLS), BF16)
    whole = pltpu.VMEM((ORDER, ORDER), F32)
    anywhere = pl.BlockSpec(memory_space=pl.ANY)
    inside = pl.BlockSpec(memory_space=pltpu.VMEM)
    dma = pltpu.SemaphoreType.DMA
    out = jax.ShapeDtypeStruct((ORDER, COLS), F32)
    return pl.pallas_call(
        kernel,
        out_shape=(out, out),
        in_specs=[anywhere, anywhere, anywhere, inside, inside, inside, inside],
        out_specs=(anywhere, anywhere),
        scratch_shapes=[
            whole, whole, square, square, square, square, square, square,
            pltpu.VMEM((JUMPS, ORDER, COLS), F32), pltpu.VMEM((JUMPS, ORDER, COLS), F32),
            vector, vector, field, field, field, field, field, field, field, field, field, field, field, field,
            field, slim, slim, slim, slim,
            pltpu.VMEM((2 * BLK, ORDER), BF16), pltpu.VMEM((BLK, ORDER), F32), pltpu.VMEM((BLK, 24 * 128), F32),
            pltpu.VMEM((GROUP, BLK, GROUP * BLK), F32), pltpu.VMEM((GROUP, BLK, GROUP * BLK), F32),
            pltpu.VMEM((GROUP * BLK, GROUP * BLK), BF16), pltpu.VMEM((GROUP * BLK, GROUP * BLK), BF16),
            pltpu.VMEM((ROUNDS, GROUP, BLK, COLS), F32), pltpu.VMEM((ROUNDS, GROUP, BLK, COLS), F32),
            pltpu.VMEM((ROUNDS, GROUP, BLK, COLS), F32), pltpu.VMEM((ITERS, 8, BLK, COLS), F32),
            pltpu.VMEM((BLK, COLS), F32), pltpu.VMEM((BLK, COLS), F32),
            dma((7,)), dma((2,)), dma((JUMPS, SLOTS)), dma((JUMPS, SLOTS)), dma, dma,
            dma((ROUNDS,)), dma((ROUNDS,)), dma((ROUNDS,)), dma((ROUNDS,)), dma((ITERS, SLOTS)), dma((ITERS, SLOTS)),
        ],
        compiler_params=pltpu.CompilerParams(
            collective_id=0, has_side_effects=True, vmem_limit_bytes=63 * 1024 * 1024
        ),
        name="dual_solve",
    )(
        applied_loads, local_inverse, schur_block, coarse_modes, coarse_rows, ids,
        iface_rows.reshape(1, ORDER),
    )


def solution(mesh):
    return jax.shard_map(
        on_device,
        mesh=mesh,
        in_specs=(
            P("sub", None),
            P("sub", None),
            P("sub", None),
            P("sub", None),
            P("sub", None),
            P(),
            P("sub", None),
            P("sub", None, None),
        ),
        out_specs=(P("sub", None), P("sub", None)),
        check_vma=False,
    )
```

time: 1000 us -> 148 us (0.15)
  waiting for transfers between devices: 346 us -> 0 us
  blocking collectives: 284 us -> 0 us
  Pallas kernels: 0 us -> 140 us
  starting transfers between devices: 135 us -> 0 us
  other arithmetic: 94.7 us -> 0.71 us
  matrix products: 71.5 us -> 0 us
  local copies, waits for them, and re-layouts: 47.4 us -> 6.23 us
  between operations: 15.4 us -> 0.65 us
    all_gather x3 -> x0, waiting for transfers between devices: 309 us -> none  [on_device(): lax.all_gather(projected, 'sub', axis=0, tiled=True)]
    psum x3 -> x0, blocking collectives: 284 us -> none  [on_device(): lax.psum((jnp.sum(residual * image_field, axis=0), jnp.sum(image_field *...]
    pallas_call x0 -> x1, Pallas kernels: none -> 140 us  [on_device(): pl.pallas_call(kernel, out_shape=(out, out), in_specs=[anywhere, anywhere...]
    ppermute x42 -> x0, starting transfers between devices: 135 us -> none  [shifted(): lax.ppermute(value, axis, [(source, source + steps) for source in range(l...]
    scatter-add x7 -> x0, other arithmetic: 71.9 us -> none  [interface_jump(): return jnp.zeros_like(source_field).at[row_lists].add(difference)]
    dot_general x16 -> x0, matrix products: 71.5 us -> none  [apply_block(): jnp.dot(matrix, operand, precision=HIGHEST_PRECISION, preferred_element_t...]
    ppermute x42 -> x0, waiting for transfers between devices: 36.9 us -> none  [shifted(): lax.ppermute(value, axis, [(source, source + steps) for source in range(l...]
    gather x8 -> x0, local copies, waits for them, and re-layouts: 32.1 us -> none  [the longest x7 19.9 us: interface_jump(): outgoing = jnp.where(usable[:, :, None], source_field[row_lists], 0.0)]
  transfers between devices with their start and end apart: 45 -> 0, of which waited for: 20 -> 0; matrix products, arithmetic and copies ran while one was open for 2% -> 0% of each run, Pallas kernels for 0% -> 0%
where the time goes in v1:
time: 148 us; the launch traced here: 147 us
  Pallas kernels  140 us (95%)
  local copies, waits for them, and re-layouts  6.23 us (4%)
    pallas_call x1, Pallas kernels, on_device(): pl.pallas_call(kernel, out_shape=(out, out), in_specs=[anywhere, anywhere...  140 us
    unnamed x4, local copies, waits for them, and re-layouts  4.71 us

profile of v1, /device:TPU:1, one launch (start us, length us, event | category | flops | bytes accessed | tf_op | source)
XLA Modules:
  0.0 147.5 jit_solution(7292606795719093264)
XLA Ops:
  0.6 0.7 reduce
  1.3 0.7 reshape.15.iface_in
  2.0 0.8 copy.10
  3.0 0.8 reshape.14.ids_in
  3.8 139.9 %dual_solve.1 = (f32[1152,128]{1,0:T(8,128)}, f32[1152,128]{1,0:T(8,128)}) custom-call(f32[1152,128]{1,0:T(8,128)} %loads_hbm.1, f32[1152,1152]{1,0:T(8,128)} %inverse_hbm.1, f32[1152,1152]{1,0:T(8,128)} %schur_hbm.1, f32[12,1152]{1,0:T(8,128)} %modes_in.1, f32[12,3072]{1,0:T(8,128)} %rows_in.1, s32[16,1,256]{2,1,0:T(1,128)} %reshape.14.ids_in, ...), custom_call_target="tpu_custom_call" | custom-call | tf_op jit(solution)/shard_map/dual_solve/pallas_call | solution.py:489
  143.7 1.9 %copy.15 = f32[1152,128]{1,0:T(8,128)} copy(f32[1152,128]{1,0:T(8,128)} %get-tuple-element.4) | data formatting | bytes 1179648
  145.6 1.9 %copy.16 = f32[1152,128]{1,0:T(8,128)} copy(f32[1152,128]{1,0:T(8,128)} %get-tuple-element.5) | data formatting | bytes 1179648
  (2 shorter events, 0.1 us)

commit v2 on v1

--- a/solution.py
+++ b/solution.py
@@ -20,7 +20,6 @@
 GROUP = 16
 BLK = 16
 JUMPS = 2 + 2 * ITERS
-ROUNDS = ITERS + 1
 TILE = 384
 F32 = jnp.float32
 BF16 = jnp.bfloat16
@@ -44,12 +43,12 @@
 
 def kernel(
     loads_hbm, inverse_hbm, schur_hbm, modes_in, rows_in, ids_in, iface_in,
-    mult_hbm, disp_hbm,
+    mult_hbm, disp_hbm, direction_hbm, resp_hbm, step_out,
     stage_k, stage_s, k_hi, k_lo, s_hi, s_lo, scatter_m, gather_m,
     out_buf, in_buf, vec, vec2, cnt, phi_t, u, w, lifted, rw, smoothed, response, gap, disp, mult, og,
     gw, m_hi, m_lo, em_hi, em_lo, ps, phi_pad, c_pad, c_send, c_recv, cb_hi, cb_lo,
-    pbuf, part, rbuf, cst, coarse, mult_co,
-    load_sem, out_sem, jump_send, jump_recv, c_ssem, c_rsem, p_ssem, p_rsem, q_ssem, q_rsem, n_ssem, n_rsem,
+    pbuf, part, rbuf, cst, coarse, mult_co, sums_z, sums_p,
+    load_sem, out_sem, jump_send, jump_recv, c_ssem, c_rsem, p_ssem, p_rsem, q_ssem, q_rsem, n_ssem, n_rsem, last_ssem, last_rsem,
 ):
     me = lax.axis_index("sub")
     core = lax.rem(me, 2)
@@ -98,23 +97,98 @@
         def _(slot=slot):
             pl.semaphore_signal(barrier, inc=1, device_id=(me + OFFSETS[slot],), device_id_type=MESH)
 
-    row_of = iface_in[...]
-
     @pl.loop(0, 9)
     def _(i):
         rows = pl.ds(pl.multiple_of(i * 128, 128), 128)
-        ids = lax.broadcasted_iota(jnp.int32, (128, ORDER), 0) + i * 128
-        scatter_m[rows, :] = jnp.where(ids == row_of, 1.0, 0.0).astype(BF16)
         across = jnp.broadcast_to(iface_in[:, rows], (128, 128)).T
         for c in range(9):
             lanes = lax.broadcasted_iota(jnp.int32, (128, 128), 1) + c * 128
             gather_m[rows, c * 128:(c + 1) * 128] = jnp.where(lanes == across, 1.0, 0.0).astype(BF16)
 
-    phi_pad[...] = jnp.zeros_like(phi_pad)
-    phi_pad[0:MODES_SUB, :] = modes_in[...]
-    for c in range(9):
-        piece = phi_pad[:, c * 128:(c + 1) * 128]
-        phi_t[c * 128:(c + 1) * 128, :] = jnp.concatenate([piece] * 8, axis=0).T
+    def load_vec(ref_to, value):
+        high, low = split(value)
+        ref_to[:, :COLS] = high
+        ref_to[:, COLS:] = low
+
+    def product(high_ref, low_ref, vec_ref, into):
+        @pl.loop(0, ORDER // TILE)
+        def _(i):
+            rows = pl.ds(pl.multiple_of(i * TILE, TILE), TILE)
+            total = dot(high_ref[rows, :], vec_ref[...]) + dot(low_ref[rows, :], vec_ref[...])
+            into[rows, :] = fold(total)
+
+    def jump_copy(jump, slot):
+        return pltpu.make_async_remote_copy(
+            src_ref=out_buf.at[jump, pl.ds(slot * IFACE, IFACE)],
+            dst_ref=in_buf.at[jump, pl.ds((slot ^ 1) * IFACE, IFACE)],
+            send_sem=jump_send.at[jump, slot],
+            recv_sem=jump_recv.at[jump, slot ^ 1],
+            device_id=(me + OFFSETS[slot],),
+            device_id_type=MESH,
+        )
+
+    def jump_arrival(jump, slot):
+        return pltpu.make_async_remote_copy(
+            src_ref=out_buf.at[jump, pl.ds(slot * IFACE, IFACE)],
+            dst_ref=in_buf.at[jump, pl.ds(slot * IFACE, IFACE)],
+            send_sem=jump_send.at[jump, slot],
+            recv_sem=jump_recv.at[jump, slot],
+            device_id=(me + OFFSETS[slot],),
+            device_id_type=MESH,
+        )
+
+    def send_slot(jump, slot):
+        @pl.when(has(slot))
+        def _():
+            jump_copy(jump, slot).start()
+
+    def scattered(jump, own):
+        for first, second in ((0, 1), (4, 5), (2, 3)):
+            for slot in (first, second):
+                @pl.when(has(slot))
+                def _(slot=slot):
+                    jump_arrival(jump, slot).wait_recv()
+            pair = slice(first * IFACE, (second + 1) * IFACE)
+            high, low = split(in_buf[jump, pair, :])
+            vec[pair, :COLS] = high
+            vec[pair, COLS:] = low
+
+            def body(i, carry, pair=pair):
+                rows = pl.ds(pl.multiple_of(i * TILE, TILE), TILE)
+                own[rows, :] = own[rows, :] - fold(dot(scatter_m[rows, pair], vec[pair, :]))
+                return carry
+
+            lax.fori_loop(0, ORDER // TILE, body, 0)
+
+    def gather_send(jump, vec_ref):
+        for first, second in PAIRS:
+            rows = slice(first * IFACE, (second + 1) * IFACE)
+            out_buf[jump, rows, :] = fold(dot(gather_m[rows, :], vec_ref[...]))
+            send_slot(jump, first)
+            send_slot(jump, second)
+
+    load_copy.wait()
+    load_vec(vec, disp[...])
+    for i in range(3):
+        copies_k[i].wait()
+        rows = slice(i * TILE, (i + 1) * TILE)
+        high, low = split(stage_k[rows, :])
+        k_hi[rows, :] = high
+        k_lo[rows, :] = low
+        disp[rows, :] = fold(dot(high, vec[...]) + dot(low, vec[...]))
+    load_vec(vec2, disp[...])
+    pl.semaphore_wait(barrier, 2 * (GROUP - 1) + present)
+    gather_send(1, vec2)
+
+    for slot in range(SLOTS):
+        @pl.when(jnp.logical_not(has(slot)))
+        def _(slot=slot):
+            for j in range(JUMPS):
+                in_buf[j, slot * IFACE:(slot + 1) * IFACE, :] = jnp.zeros((IFACE, COLS), F32)
+            for n in range(ITERS):
+                cst[n, slot + 1] = jnp.zeros((BLK, COLS), F32)
+    for n in range(ITERS):
+        cst[n, 7] = jnp.zeros((BLK, COLS), F32)
 
     c_pad[...] = jnp.zeros_like(c_pad)
     c_pad[0:MODES_SUB, :] = rows_in[...]
@@ -139,100 +213,6 @@
                     total = jnp.where(keep, 1.0, total)
                 c_send[target, octet * 8:(octet + 1) * 8, half * 128:(half + 1) * 128] = total
 
-    ones = jnp.ones((ORDER, COLS), BF16)
-    cnt[...] = dot(scatter_m[...], ones)
-
-    for slot in range(SLOTS):
-        @pl.when(jnp.logical_not(has(slot)))
-        def _(slot=slot):
-            for j in range(JUMPS):
-                in_buf[j, slot * IFACE:(slot + 1) * IFACE, :] = jnp.zeros((IFACE, COLS), F32)
-            for n in range(ITERS):
-                cst[n, slot + 1] = jnp.zeros((BLK, COLS), F32)
-    for n in range(ITERS):
-        cst[n, 7] = jnp.zeros((BLK, COLS), F32)
-
-    def load_vec(ref_to, value):
-        high, low = split(value)
-        ref_to[:, :COLS] = high
-        ref_to[:, COLS:] = low
-
-    def product(high_ref, low_ref, vec_ref, into):
-        @pl.loop(0, ORDER // TILE)
-        def _(i):
-            rows = pl.ds(pl.multiple_of(i * TILE, TILE), TILE)
-            total = dot(high_ref[rows, :], vec_ref[...]) + dot(low_ref[rows, :], vec_ref[...])
-            into[rows, :] = fold(total)
-
-    def scattered(jump, own):
-        load_vec(vec, in_buf[jump])
-
-        def body(i, carry):
-            rows = pl.ds(pl.multiple_of(i * TILE, TILE), TILE)
-            own[rows, :] = own[rows, :] - fold(dot(scatter_m[rows, :], vec[...]))
-            return carry
-
-        lax.fori_loop(0, ORDER // TILE, body, 0)
-
-    def jump_copy(jump, slot):
-        return pltpu.make_async_remote_copy(
-            src_ref=out_buf.at[jump, pl.ds(slot * IFACE, IFACE)],
-            dst_ref=in_buf.at[jump, pl.ds((slot ^ 1) * IFACE, IFACE)],
-            send_sem=jump_send.at[jump, slot],
-            recv_sem=jump_recv.at[jump, slot ^ 1],
-            device_id=(me + OFFSETS[slot],),
-            device_id_type=MESH,
-        )
-
-    def jump_arrival(jump, slot):
-        return pltpu.make_async_remote_copy(
-            src_ref=out_buf.at[jump, pl.ds(slot * IFACE, IFACE)],
-            dst_ref=in_buf.at[jump, pl.ds(slot * IFACE, IFACE)],
-            send_sem=jump_send.at[jump, slot],
-            recv_sem=jump_recv.at[jump, slot],
-            device_id=(me + OFFSETS[slot],),
-            device_id_type=MESH,
-        )
-
-    def send_slot(jump, slot):
-        @pl.when(has(slot))
-        def _():
-            jump_copy(jump, slot).start()
-
-    def await_jump(jump):
-        for slot in range(SLOTS):
-            @pl.when(has(slot))
-            def _(slot=slot):
-                jump_arrival(jump, slot).wait_recv()
-
-    def gather_send(jump, vec_ref):
-        for first, second in PAIRS:
-            rows = slice(first * IFACE, (second + 1) * IFACE)
-            out_buf[jump, rows, :] = fold(dot(gather_m[rows, :], vec_ref[...]))
-            send_slot(jump, first)
-            send_slot(jump, second)
-
-    load_copy.wait()
-    load_vec(vec, disp[...])
-    for i in range(3):
-        copies_k[i].wait()
-        rows = slice(i * TILE, (i + 1) * TILE)
-        high, low = split(stage_k[rows, :])
-        k_hi[rows, :] = high
-        k_lo[rows, :] = low
-    product(k_hi, k_lo, vec, disp)
-    load_vec(vec, disp[...])
-    pl.semaphore_wait(barrier, 2 * (GROUP - 1) + present)
-    gather_send(1, vec)
-
-    load_vec(vec2, phi_t[...])
-    lane_block = lax.div(lax.broadcasted_iota(jnp.int32, (IFACE, COLS), 1), BLK)
-    for slot in range(SLOTS):
-        rows = slice(slot * IFACE, (slot + 1) * IFACE)
-        value = fold(dot(gather_m[rows, :], vec2[...]))
-        out_buf[0, rows, :] = jnp.where(lane_block == 1 + (slot ^ 1), value, 0.0)
-        send_slot(0, slot)
-
     def send_coarse(step, carry):
         peer = lax.rem(yx + step, GROUP)
         pltpu.make_async_remote_copy(
@@ -243,6 +223,23 @@
 
     lax.fori_loop(1, GROUP, send_coarse, 0)
     c_recv[pl.ds(yx, 1)] = c_send[pl.ds(yx, 1)]
+
+    phi_pad[...] = jnp.zeros_like(phi_pad)
+    phi_pad[0:MODES_SUB, :] = modes_in[...]
+    for c in range(9):
+        piece = phi_pad[:, c * 128:(c + 1) * 128]
+        phi_t[c * 128:(c + 1) * 128, :] = jnp.concatenate([piece] * 8, axis=0).T
+
+    row_of = iface_in[...]
+
+    @pl.loop(0, 9)
+    def _(i):
+        rows = pl.ds(pl.multiple_of(i * 128, 128), 128)
+        ids = lax.broadcasted_iota(jnp.int32, (128, ORDER), 0) + i * 128
+        scatter_m[rows, :] = jnp.where(ids == row_of, 1.0, 0.0).astype(BF16)
+
+    ones = jnp.ones((ORDER, COLS), BF16)
+    cnt[...] = dot(scatter_m[...], ones)
 
     for i in range(3):
         copies_s[i].wait()
@@ -259,41 +256,52 @@
         ps[0:BLK, lanes] = high
         ps[BLK:, lanes] = low
 
-    await_jump(0)
-    lane = lax.broadcasted_iota(jnp.int32, (ORDER, COLS), 1)
-    rw[...] = jnp.where(lane < BLK, phi_t[...] * cnt[...], 0.0)
-    scattered(0, rw)
-    load_vec(vec2, rw[...])
-    product(k_hi, k_lo, vec2, rw)
-    high, low = split(rw[...])
-    m_hi[...] = high
-    m_lo[...] = low
-    vec2[:, :COLS] = high
-    vec2[:, COLS:] = low
-    for i in range(3):
-        rows = slice(i * TILE, (i + 1) * TILE)
-        total = dot(gather_m[rows, :], vec2[...])
-        em_hi[rows, :] = total[:, :COLS].astype(BF16)
-        em_lo[rows, :] = total[:, COLS:].astype(BF16)
-
-    pltpu.make_async_remote_copy(
-        src_ref=c_send.at[pl.ds(0, GROUP - 1)], dst_ref=c_recv.at[pl.ds(0, GROUP - 1)], send_sem=c_ssem, recv_sem=c_rsem,
-        device_id=(along_plane(lax.rem(yx + 1, GROUP)),), device_id_type=MESH,
-    ).wait()
-    high, low = split(c_recv[...].reshape(GROUP * BLK, GROUP * BLK))
-    cb_hi[...] = high
-    cb_lo[...] = low
+    load_vec(vec2, phi_t[...])
+    lane_block = lax.div(lax.broadcasted_iota(jnp.int32, (IFACE, COLS), 1), BLK)
+    for slot in range(SLOTS):
+        rows = slice(slot * IFACE, (slot + 1) * IFACE)
+        value = fold(dot(gather_m[rows, :], vec2[...]))
+        out_buf[0, rows, :] = jnp.where(lane_block == 1 + (slot ^ 1), value, 0.0)
 
     smoothed[...] = jnp.zeros_like(smoothed)
     response[...] = jnp.zeros_like(response)
     gap[...] = jnp.zeros_like(gap)
     mult[...] = jnp.zeros_like(mult)
+    og[...] = jnp.zeros_like(og)
     coarse[...] = jnp.zeros_like(coarse)
     mult_co[...] = jnp.zeros_like(mult_co)
-
-    await_jump(1)
     u[...] = cnt[...] * disp[...]
     scattered(1, u)
+
+    def coarse_blocks():
+        pltpu.make_async_remote_copy(
+            src_ref=c_send.at[pl.ds(0, GROUP - 1)], dst_ref=c_recv.at[pl.ds(0, GROUP - 1)],
+            send_sem=c_ssem, recv_sem=c_rsem,
+            device_id=(along_plane(lax.rem(yx + 1, GROUP)),), device_id_type=MESH,
+        ).wait()
+        high, low = split(c_recv[...].reshape(GROUP * BLK, GROUP * BLK))
+        cb_hi[...] = high
+        cb_lo[...] = low
+
+    lane = lax.broadcasted_iota(jnp.int32, (ORDER, COLS), 1)
+
+    def coarse_response():
+        rw[...] = jnp.where(lane < BLK, phi_t[...] * cnt[...], 0.0)
+        scattered(0, rw)
+        load_vec(vec2, rw[...])
+        product(k_hi, k_lo, vec2, rw)
+        high, low = split(rw[...])
+        m_hi[...] = high
+        m_lo[...] = low
+        vec2[:, :COLS] = high
+        vec2[:, COLS:] = low
+
+        @pl.loop(0, ORDER // TILE)
+        def _(i):
+            rows = pl.ds(pl.multiple_of(i * TILE, TILE), TILE)
+            total = dot(gather_m[rows, :], vec2[...])
+            em_hi[rows, :] = total[:, :COLS].astype(BF16)
+            em_lo[rows, :] = total[:, COLS:].astype(BF16)
 
     def first_round(n):
         load_vec(vec, u[...])
@@ -363,11 +371,18 @@
 
     def sweep(n, carry):
         first_round(n)
+
+        @pl.when(n == 0)
+        def _():
+            for slot in range(SLOTS):
+                send_slot(0, slot)
+
         product(s_hi, s_lo, vec, w)
         load_vec(vec2, w[...])
         gather_send(2 + 2 * n, vec2)
+        pl.when(n == 0)(coarse_blocks)
         second_round(n)
-        await_jump(2 + 2 * n)
+        pl.when(n == 0)(coarse_response)
         lifted[...] = cnt[...] * w[...]
         scattered(2 + 2 * n, lifted)
         total, step = sums(n)
@@ -411,7 +426,6 @@
 
         lax.fori_loop(0, ORDER // TILE, body, 0)
         u[...] = cnt[...] * response[...]
-        await_jump(jump)
         scattered(jump, u)
         return carry
 
@@ -420,24 +434,52 @@
         mult_co[...] = mult_co[...] + step * coarse[...]
         disp[...] = disp[...] - step * response[...]
 
-    og[...] = jnp.zeros_like(og)
     lax.fori_loop(0, ITERS, sweep, 0)
 
-    first_round(ITERS)
+    row = lax.broadcasted_iota(jnp.int32, (8, COLS), 0)
+    upper = jnp.sum(gap[...] * u[...], axis=0, keepdims=True)
+    lower = jnp.sum(u[...] * u[...], axis=0, keepdims=True)
+    sums_z[pl.ds(zc, 1)] = jnp.where(row == 0, upper, jnp.where(row == 1, lower, 0.0))[None]
+
+    def sums_copy(buffer, place, target, which):
+        return pltpu.make_async_remote_copy(
+            src_ref=buffer.at[place], dst_ref=buffer.at[place], send_sem=last_ssem.at[which], recv_sem=last_rsem.at[which],
+            device_id=(target,), device_id_type=MESH,
+        )
+
+    def sums_whole(buffer, which):
+        return whole(buffer.at[pl.ds(0, GROUP - 1)], buffer.at[pl.ds(0, GROUP - 1)], last_ssem.at[which], last_rsem.at[which])
+
+    def send_z(turn, carry):
+        sums_copy(sums_z, zc, along_z(lax.rem(zc + turn, GROUP)), 0).start()
+        return carry
+
+    lax.fori_loop(1, GROUP, send_z, 0)
+    out_r = pltpu.make_async_copy(response, resp_hbm, out_sem.at[0])
+    out_r.start()
+    out_d = pltpu.make_async_copy(disp, disp_hbm, out_sem.at[1])
+    out_d.start()
+    sums_whole(sums_z, 0).wait_recv()
+    sums_p[pl.ds(yx, 1)] = jnp.sum(sums_z[...], axis=0)[None]
+
+    def send_p(turn, carry):
+        sums_copy(sums_p, yx, along_plane(lax.rem(yx + turn, GROUP)), 1).start()
+        return carry
+
+    lax.fori_loop(1, GROUP, send_p, 0)
+
     high, low = split(jnp.where(lane < BLK, phi_t[...], 0.0))
     m_hi[...] = high
     m_lo[...] = low
-    second_round(ITERS)
-    total, step = sums(ITERS)
-    update(step)
-    out_d = pltpu.make_async_copy(disp, disp_hbm, out_sem.at[0])
-    out_d.start()
-    padded = jnp.concatenate([mult_co[...], jnp.zeros((COLS - BLK, COLS), F32)], axis=0)
-    high, low = split(padded)
-    both = jnp.concatenate([high, low], axis=1)
-    mult[...] = mult[...] + fold(dot(m_hi[...], both) + dot(m_lo[...], both))
-    out_m = pltpu.make_async_copy(mult, mult_hbm, out_sem.at[1])
+    blank = jnp.zeros((COLS - BLK, COLS), F32)
+    for field, few in ((mult, mult_co), (smoothed, coarse)):
+        high, low = split(jnp.concatenate([few[...], blank], axis=0))
+        both = jnp.concatenate([high, low], axis=1)
+        field[...] = field[...] + fold(dot(m_hi[...], both) + dot(m_lo[...], both))
+    out_m = pltpu.make_async_copy(mult, mult_hbm, out_sem.at[2])
     out_m.start()
+    out_s = pltpu.make_async_copy(smoothed, direction_hbm, out_sem.at[3])
+    out_s.start()
 
     for slot in range(SLOTS):
         @pl.when(has(slot))
@@ -459,9 +501,13 @@
         q_whole(n).wait_send()
         return carry
 
-    lax.fori_loop(0, ROUNDS, rounds_left, 0)
-    out_d.wait()
-    out_m.wait()
+    lax.fori_loop(0, ITERS, rounds_left, 0)
+    sums_whole(sums_z, 0).wait_send()
+    for copy in (out_r, out_d, out_m, out_s):
+        copy.wait()
+    sums_whole(sums_p, 1).wait()
+    final = jnp.sum(sums_p[...], axis=0)
+    step_out[...] = jnp.broadcast_to(DAMPING * final[0:1] / (final[1:2] + EPSILON), (8, COLS))
 
 
 def on_device(
@@ -486,11 +532,11 @@
     inside = pl.BlockSpec(memory_space=pltpu.VMEM)
     dma = pltpu.SemaphoreType.DMA
     out = jax.ShapeDtypeStruct((ORDER, COLS), F32)
-    return pl.pallas_call(
+    base, displaced, direction, response, step = pl.pallas_call(
         kernel,
-        out_shape=(out, out),
+        out_shape=(out, out, out, out, jax.ShapeDtypeStruct((8, COLS), F32)),
         in_specs=[anywhere, anywhere, anywhere, inside, inside, inside, inside],
-        out_specs=(anywhere, anywhere),
+        out_specs=(anywhere, anywhere, anywhere, anywhere, inside),
         scratch_shapes=[
             whole, whole, square, square, square, square, square, square,
             pltpu.VMEM((JUMPS, ORDER, COLS), F32), pltpu.VMEM((JUMPS, ORDER, COLS), F32),
@@ -499,11 +545,13 @@
             pltpu.VMEM((2 * BLK, ORDER), BF16), pltpu.VMEM((BLK, ORDER), F32), pltpu.VMEM((BLK, 24 * 128), F32),
             pltpu.VMEM((GROUP, BLK, GROUP * BLK), F32), pltpu.VMEM((GROUP, BLK, GROUP * BLK), F32),
             pltpu.VMEM((GROUP * BLK, GROUP * BLK), BF16), pltpu.VMEM((GROUP * BLK, GROUP * BLK), BF16),
-            pltpu.VMEM((ROUNDS, GROUP, BLK, COLS), F32), pltpu.VMEM((ROUNDS, GROUP, BLK, COLS), F32),
-            pltpu.VMEM((ROUNDS, GROUP, BLK, COLS), F32), pltpu.VMEM((ITERS, 8, BLK, COLS), F32),
+            pltpu.VMEM((ITERS, GROUP, BLK, COLS), F32), pltpu.VMEM((ITERS, GROUP, BLK, COLS), F32),
+            pltpu.VMEM((ITERS, GROUP, BLK, COLS), F32), pltpu.VMEM((ITERS, 8, BLK, COLS), F32),
             pltpu.VMEM((BLK, COLS), F32), pltpu.VMEM((BLK, COLS), F32),
-            dma((7,)), dma((2,)), dma((JUMPS, SLOTS)), dma((JUMPS, SLOTS)), dma, dma,
-            dma((ROUNDS,)), dma((ROUNDS,)), dma((ROUNDS,)), dma((ROUNDS,)), dma((ITERS, SLOTS)), dma((ITERS, SLOTS)),
+            pltpu.VMEM((GROUP, 8, COLS), F32), pltpu.VMEM((GROUP, 8, COLS), F32),
+            dma((7,)), dma((4,)), dma((JUMPS, SLOTS)), dma((JUMPS, SLOTS)), dma, dma,
+            dma((ITERS,)), dma((ITERS,)), dma((ITERS,)), dma((ITERS,)), dma((ITERS, SLOTS)), dma((ITERS, SLOTS)),
+            dma((2,)), dma((2,)),
         ],
         compiler_params=pltpu.CompilerParams(
             collective_id=0, has_side_effects=True, vmem_limit_bytes=63 * 1024 * 1024
@@ -513,6 +561,7 @@
         applied_loads, local_inverse, schur_block, coarse_modes, coarse_rows, ids,
         iface_rows.reshape(1, ORDER),
     )
+    return base + step[0:1] * direction, displaced - step[0:1] * response
 
 
 def solution(mesh):

time: 148 us -> 138 us (0.932)
  Pallas kernels: 140 us -> 131 us
  local copies, waits for them, and re-layouts: 6.23 us -> 3.08 us
  other arithmetic: 0.71 us -> 3.44 us
    pallas_call x1, Pallas kernels: 140 us -> 131 us  [on_device(): pl.pallas_call(kernel, out_shape=(out, out, out, out, jax.ShapeDtypeStruc...]
    unnamed x4 -> x2, local copies, waits for them, and re-layouts: 4.71 us -> 0.87 us
    sub x0 -> x1, other arithmetic: none -> 2.72 us  [on_device(): return (base + step[0:1] * direction, displaced - step[0:1] * response)]
where the time goes in v2:
time: 138 us
  Pallas kernels  131 us (95%)
  other arithmetic  3.44 us (2%)
  local copies, waits for them, and re-layouts  3.08 us (2%)
    pallas_call x1, Pallas kernels, on_device(): pl.pallas_call(kernel, out_shape=(out, out, out, out, jax.ShapeDtypeStruc...  131 us

profile of v2, /device:TPU:1, one launch (start us, length us, event | category | flops | bytes accessed | tf_op | source)
XLA Modules:
  0.0 138.0 jit_solution(1260771851680980283)
XLA Ops:
  0.6 0.7 reduce
  1.3 0.7 reshape.15.iface_in
  2.0 0.8 copy.10
  3.0 0.8 reshape.14.ids_in
  3.8 130.8 %dual_solve.1 = (f32[1152,128]{1,0:T(8,128)}, f32[1152,128]{1,0:T(8,128)}, f32[1152,128]{1,0:T(8,128)}, f32[1152,128]{1,0:T(8,128)}, f32[8,128]{1,0:T(8,128)}) custom-call(f32[1152,128]{1,0:T(8,128)} %loads_hbm.1, f32[1152,1152]{1,0:T(8,128)} %inverse_hbm.1, f32[1152,1152]{1,0:T(8,128)} %schur_hbm.1, f32[12,1152]{1,0:T(8,128)} %modes_in.1, ...), custom_call_target="tpu_custom_call" | custom-call | tf_op jit(solution)/shard_map/dual_solve/pallas_call | solution.py:535
  134.6 0.7 slice_bitcast_fusion
  135.2 2.7 %multiply_subtract_fusion = (f32[1152,128]{1,0:T(8,128)}, f32[1152,128]{1,0:T(8,128)}) fusion(f32[1152,128]{1,0:T(8,128)} %get-tuple-element.10, f32[1152,128]{1,0:T(8,128)} %get-tuple-element.11, f32[128]{0:T(128)S(1)} %slice_bitcast_fusion, f32[1152,128]{1,0:T(8,128)} %get-tuple-element.7, f32[1152,128]{1,0:T(8,128)} %get-tuple-element.9), kind=kLoop, calls=%fused_computation | loop fusion | flops 589824 | bytes 3539456 | tf_op jit(solution)/shard_map/sub | solution.py:564
  (2 shorter events, 0.1 us)

commit v3 on v2

--- a/solution.py
+++ b/solution.py
@@ -19,7 +19,7 @@
 EXTENTS = (4, 4, 16)
 GROUP = 16
 BLK = 16
-JUMPS = 2 + 2 * ITERS
+JUMPS = 1 + 2 * ITERS
 TILE = 384
 F32 = jnp.float32
 BF16 = jnp.bfloat16
@@ -47,13 +47,14 @@
     stage_k, stage_s, k_hi, k_lo, s_hi, s_lo, scatter_m, gather_m,
     out_buf, in_buf, vec, vec2, cnt, phi_t, u, w, lifted, rw, smoothed, response, gap, disp, mult, og,
     gw, m_hi, m_lo, em_hi, em_lo, ps, phi_pad, c_pad, c_send, c_recv, cb_hi, cb_lo,
-    pbuf, part, rbuf, cst, coarse, mult_co, sums_z, sums_p,
-    load_sem, out_sem, jump_send, jump_recv, c_ssem, c_rsem, p_ssem, p_rsem, q_ssem, q_rsem, n_ssem, n_rsem, last_ssem, last_rsem,
+    pbuf, part, rbuf, cst, coarse, mult_co, sums_z, sums_p, iface_row, ids_pad, phi_out, phi_near, phi_all,
+    load_sem, out_sem, jump_send, jump_recv, c_ssem, c_rsem, p_ssem, p_rsem, q_ssem, q_rsem, n_ssem, n_rsem, last_ssem, last_rsem, phi_ssem, phi_rsem,
 ):
     me = lax.axis_index("sub")
     core = lax.rem(me, 2)
     yx = lax.rem(lax.div(me, 2), GROUP)
-    zc = lax.div(me, 32) * 2 + core
+    layer = lax.div(me, 32)
+    zc = core * 8 + layer
 
     def has(slot):
         axis = slot // 2
@@ -61,10 +62,25 @@
         return place < EXTENTS[axis] - 1 if slot % 2 == 0 else place > 0
 
     def along_z(index):
-        return lax.div(index, 2) * 32 + yx * 2 + lax.rem(index, 2)
+        return lax.rem(index, 8) * 32 + yx * 2 + lax.div(index, 8)
 
     def along_plane(index):
         return lax.div(me, 32) * 32 + index * 2 + core
+
+    peers_z = []
+    for far in (4, 3, 5, 2, 6, 1, 7, 0):
+        for other in (0, 1):
+            if far or other:
+                place_z = lax.rem(layer + far, 8)
+                place_c = lax.rem(core + other, 2)
+                peers_z.append((place_c * 8 + place_z, place_z * 32 + yx * 2 + place_c))
+    peers_p = []
+    place_x, place_y = lax.rem(yx, 4), lax.div(yx, 4)
+    for far_y, far_x in sorted(
+        ((a, b) for a in range(4) for b in range(4) if a or b), key=lambda pair: -min(pair[0], 4 - pair[0]) - min(pair[1], 4 - pair[1])
+    ):
+        index = lax.rem(place_y + far_y, 4) * 4 + lax.rem(place_x + far_x, 4)
+        peers_p.append((index, layer * 32 + index * 2 + core))
 
     copies_k, copies_s = [], []
     load_copy = pltpu.make_async_copy(loads_hbm, disp, load_sem.at[6])
@@ -76,9 +92,7 @@
         copies_k.append(copy)
     for i in range(3):
         part_rows = pl.ds(i * TILE, TILE)
-        copy = pltpu.make_async_copy(schur_hbm.at[part_rows], stage_s.at[part_rows], load_sem.at[3 + i])
-        copy.start()
-        copies_s.append(copy)
+        copies_s.append(pltpu.make_async_copy(schur_hbm.at[part_rows], stage_s.at[part_rows], load_sem.at[3 + i]))
 
     barrier = pltpu.get_barrier_semaphore()
 
@@ -97,10 +111,13 @@
         def _(slot=slot):
             pl.semaphore_signal(barrier, inc=1, device_id=(me + OFFSETS[slot],), device_id_type=MESH)
 
+    for slot in range(SLOTS):
+        iface_row[0:1, slot * IFACE:(slot + 1) * IFACE] = iface_in[0, slot:slot + 1, :]
+
     @pl.loop(0, 9)
     def _(i):
         rows = pl.ds(pl.multiple_of(i * 128, 128), 128)
-        across = jnp.broadcast_to(iface_in[:, rows], (128, 128)).T
+        across = jnp.broadcast_to(iface_row[0:1, rows], (128, 128)).T
         for c in range(9):
             lanes = lax.broadcasted_iota(jnp.int32, (128, 128), 1) + c * 128
             gather_m[rows, c * 128:(c + 1) * 128] = jnp.where(lanes == across, 1.0, 0.0).astype(BF16)
@@ -133,6 +150,17 @@
             dst_ref=in_buf.at[jump, pl.ds(slot * IFACE, IFACE)],
             send_sem=jump_send.at[jump, slot],
             recv_sem=jump_recv.at[jump, slot],
+            device_id=(me + OFFSETS[slot],),
+            device_id_type=MESH,
+        )
+
+    def phi_copy(slot, arriving):
+        place = slot if arriving else slot ^ 1
+        return pltpu.make_async_remote_copy(
+            src_ref=phi_out.at[slot],
+            dst_ref=phi_near.at[place],
+            send_sem=phi_ssem.at[slot],
+            recv_sem=phi_rsem.at[place],
             device_id=(me + OFFSETS[slot],),
             device_id_type=MESH,
         )
@@ -171,6 +199,7 @@
     load_vec(vec, disp[...])
     for i in range(3):
         copies_k[i].wait()
+        copies_s[i].start()
         rows = slice(i * TILE, (i + 1) * TILE)
         high, low = split(stage_k[rows, :])
         k_hi[rows, :] = high
@@ -178,11 +207,12 @@
         disp[rows, :] = fold(dot(high, vec[...]) + dot(low, vec[...]))
     load_vec(vec2, disp[...])
     pl.semaphore_wait(barrier, 2 * (GROUP - 1) + present)
-    gather_send(1, vec2)
+    gather_send(0, vec2)
 
     for slot in range(SLOTS):
         @pl.when(jnp.logical_not(has(slot)))
         def _(slot=slot):
+            phi_near[slot] = jnp.zeros((BLK, GROUP * BLK), F32)
             for j in range(JUMPS):
                 in_buf[j, slot * IFACE:(slot + 1) * IFACE, :] = jnp.zeros((IFACE, COLS), F32)
             for n in range(ITERS):
@@ -192,10 +222,15 @@
 
     c_pad[...] = jnp.zeros_like(c_pad)
     c_pad[0:MODES_SUB, :] = rows_in[...]
+    ids_pad[...] = jnp.full_like(ids_pad, -1)
+    ids_pad[:, 0:MODES_SUB] = ids_in[...]
     for half in range(2):
         @pl.loop(0, GROUP)
         def _(target, half=half):
-            ids = ids_in[target, :, half * 128:(half + 1) * 128]
+            ids = ids_pad[pl.ds(target * 2 + half, 8, stride=32), :]
+            ids = jnp.take_along_axis(ids, lax.bitwise_and(lax.broadcasted_iota(jnp.int32, (8, 128), 1), 15), axis=1)
+            mine = lax.shift_right_arithmetic(lax.broadcasted_iota(jnp.int32, (8, 128), 1), 4) == lax.broadcasted_iota(jnp.int32, (8, 128), 0)
+            ids = jnp.sum(jnp.where(mine, ids, 0), axis=0, keepdims=True)
             ids = jnp.broadcast_to(ids, (8, 128))
             tile_id = lax.shift_right_arithmetic(ids, 7)
             lane_id = lax.bitwise_and(ids, 127)
@@ -230,7 +265,7 @@
         piece = phi_pad[:, c * 128:(c + 1) * 128]
         phi_t[c * 128:(c + 1) * 128, :] = jnp.concatenate([piece] * 8, axis=0).T
 
-    row_of = iface_in[...]
+    row_of = iface_row[0:1, :]
 
     @pl.loop(0, 9)
     def _(i):
@@ -256,12 +291,14 @@
         ps[0:BLK, lanes] = high
         ps[BLK:, lanes] = low
 
-    load_vec(vec2, phi_t[...])
-    lane_block = lax.div(lax.broadcasted_iota(jnp.int32, (IFACE, COLS), 1), BLK)
+    total = dot(both, scatter_m[...])
+    total = total[:BLK] + total[BLK:]
     for slot in range(SLOTS):
-        rows = slice(slot * IFACE, (slot + 1) * IFACE)
-        value = fold(dot(gather_m[rows, :], vec2[...]))
-        out_buf[0, rows, :] = jnp.where(lane_block == 1 + (slot ^ 1), value, 0.0)
+        phi_out[slot, :, 0:IFACE] = total[:, slot * IFACE:(slot + 1) * IFACE]
+
+        @pl.when(has(slot))
+        def _(slot=slot):
+            phi_copy(slot, False).start()
 
     smoothed[...] = jnp.zeros_like(smoothed)
     response[...] = jnp.zeros_like(response)
@@ -271,7 +308,7 @@
     coarse[...] = jnp.zeros_like(coarse)
     mult_co[...] = jnp.zeros_like(mult_co)
     u[...] = cnt[...] * disp[...]
-    scattered(1, u)
+    scattered(0, u)
 
     def coarse_blocks():
         pltpu.make_async_remote_copy(
@@ -286,8 +323,20 @@
     lane = lax.broadcasted_iota(jnp.int32, (ORDER, COLS), 1)
 
     def coarse_response():
+        phi_all[...] = jnp.zeros_like(phi_all)
+        for slot in range(SLOTS):
+            @pl.when(has(slot))
+            def _(slot=slot):
+                phi_copy(slot, True).wait_recv()
+
+            phi_all[(slot + 1) * BLK:(slot + 2) * BLK, slot * IFACE:(slot + 1) * IFACE] = phi_near[slot, :, 0:IFACE]
+        high, low = split(phi_all[...])
+        both = jnp.concatenate([high, low], axis=0)
         rw[...] = jnp.where(lane < BLK, phi_t[...] * cnt[...], 0.0)
-        scattered(0, rw)
+        for i in range(3):
+            rows = slice(i * TILE, (i + 1) * TILE)
+            taken = lax.dot_general(scatter_m[rows, :], both, (((1,), (1,)), ((), ())), preferred_element_type=F32)
+            rw[rows, :] = rw[rows, :] - fold(taken)
         load_vec(vec2, rw[...])
         product(k_hi, k_lo, vec2, rw)
         high, low = split(rw[...])
@@ -315,14 +364,11 @@
         total = jnp.where(row == 12, upper, jnp.where(row == 13, lower, total))
         pbuf[n, pl.ds(zc, 1)] = total[None]
 
-        def send(step, carry):
+        for _, device in peers_z:
             pltpu.make_async_remote_copy(
                 src_ref=pbuf.at[n, zc], dst_ref=pbuf.at[n, zc], send_sem=p_ssem.at[n], recv_sem=p_rsem.at[n],
-                device_id=(along_z(lax.rem(zc + step, GROUP)),), device_id_type=MESH,
+                device_id=(device,), device_id_type=MESH,
             ).start()
-            return carry
-
-        lax.fori_loop(1, GROUP, send, 0)
 
     def whole(src, dst, ssem, rsem):
         return pltpu.make_async_remote_copy(
@@ -343,15 +389,11 @@
         total = fold(dot(cb_hi[...], both) + dot(cb_lo[...], both))
         part[n] = total.reshape(GROUP, BLK, COLS)
 
-        def send(step, carry):
-            peer = lax.rem(yx + step, GROUP)
+        for peer, device in peers_p:
             pltpu.make_async_remote_copy(
                 src_ref=part.at[n, peer], dst_ref=rbuf.at[n, yx], send_sem=q_ssem.at[n], recv_sem=q_rsem.at[n],
-                device_id=(along_plane(peer),), device_id_type=MESH,
+                device_id=(device,), device_id_type=MESH,
             ).start()
-            return carry
-
-        lax.fori_loop(1, GROUP, send, 0)
         rbuf[n, pl.ds(yx, 1)] = part[n, pl.ds(yx, 1)]
 
     def sums(n):
@@ -372,19 +414,14 @@
     def sweep(n, carry):
         first_round(n)
 
-        @pl.when(n == 0)
-        def _():
-            for slot in range(SLOTS):
-                send_slot(0, slot)
-
         product(s_hi, s_lo, vec, w)
         load_vec(vec2, w[...])
-        gather_send(2 + 2 * n, vec2)
+        gather_send(1 + 2 * n, vec2)
         pl.when(n == 0)(coarse_blocks)
         second_round(n)
         pl.when(n == 0)(coarse_response)
         lifted[...] = cnt[...] * w[...]
-        scattered(2 + 2 * n, lifted)
+        scattered(1 + 2 * n, lifted)
         total, step = sums(n)
         step = jnp.where(n == 0, -1.0, step)
         total = jnp.where(lax.broadcasted_iota(jnp.int32, (BLK, COLS), 0) < MODES_SUB, total, 0.0)
@@ -405,7 +442,7 @@
                 near_copy(n, slot, True).wait_recv()
         high, low = split(cst[n].reshape(8 * BLK, COLS))
         near = jnp.concatenate([high, low], axis=1)
-        jump = 3 + 2 * n
+        jump = 2 + 2 * n
         for first, second in PAIRS:
             rows = slice(first * IFACE, (second + 1) * IFACE)
             change = gw[rows, :] + fold(dot(em_hi[rows, :], near) + dot(em_lo[rows, :], near))
@@ -450,11 +487,8 @@
     def sums_whole(buffer, which):
         return whole(buffer.at[pl.ds(0, GROUP - 1)], buffer.at[pl.ds(0, GROUP - 1)], last_ssem.at[which], last_rsem.at[which])
 
-    def send_z(turn, carry):
-        sums_copy(sums_z, zc, along_z(lax.rem(zc + turn, GROUP)), 0).start()
-        return carry
-
-    lax.fori_loop(1, GROUP, send_z, 0)
+    for _, device in peers_z:
+        sums_copy(sums_z, zc, device, 0).start()
     out_r = pltpu.make_async_copy(response, resp_hbm, out_sem.at[0])
     out_r.start()
     out_d = pltpu.make_async_copy(disp, disp_hbm, out_sem.at[1])
@@ -462,11 +496,8 @@
     sums_whole(sums_z, 0).wait_recv()
     sums_p[pl.ds(yx, 1)] = jnp.sum(sums_z[...], axis=0)[None]
 
-    def send_p(turn, carry):
-        sums_copy(sums_p, yx, along_plane(lax.rem(yx + turn, GROUP)), 1).start()
-        return carry
-
-    lax.fori_loop(1, GROUP, send_p, 0)
+    for _, device in peers_p:
+        sums_copy(sums_p, yx, device, 1).start()
 
     high, low = split(jnp.where(lane < BLK, phi_t[...], 0.0))
     m_hi[...] = high
@@ -488,6 +519,7 @@
                 jump_copy(jump, slot).wait_send()
                 return carry
 
+            phi_copy(slot, False).wait_send()
             lax.fori_loop(0, JUMPS, jump_left, 0)
 
             def near_left(n, carry):
@@ -507,7 +539,7 @@
         copy.wait()
     sums_whole(sums_p, 1).wait()
     final = jnp.sum(sums_p[...], axis=0)
-    step_out[...] = jnp.broadcast_to(DAMPING * final[0:1] / (final[1:2] + EPSILON), (8, COLS))
+    step_out[...] = DAMPING * final[0:1] / (final[1:2] + EPSILON)
 
 
 def on_device(
@@ -520,9 +552,6 @@
     neighbours,
     iface_rows,
 ):
-    ids = mode_ids.reshape(DEVICES // 32, GROUP, 2, MODES_SUB).transpose(1, 0, 2, 3)
-    ids = jnp.pad(ids, ((0, 0), (0, 0), (0, 0), (0, BLK - MODES_SUB)), constant_values=-1)
-    ids = ids.reshape(GROUP, 1, GROUP * BLK)
     field = pltpu.VMEM((ORDER, COLS), F32)
     square = pltpu.VMEM((ORDER, ORDER), BF16)
     vector = pltpu.VMEM((ORDER, 2 * COLS), BF16)
@@ -534,7 +563,7 @@
     out = jax.ShapeDtypeStruct((ORDER, COLS), F32)
     base, displaced, direction, response, step = pl.pallas_call(
         kernel,
-        out_shape=(out, out, out, out, jax.ShapeDtypeStruct((8, COLS), F32)),
+        out_shape=(out, out, out, out, jax.ShapeDtypeStruct((1, COLS), F32)),
         in_specs=[anywhere, anywhere, anywhere, inside, inside, inside, inside],
         out_specs=(anywhere, anywhere, anywhere, anywhere, inside),
         scratch_shapes=[
@@ -549,19 +578,20 @@
             pltpu.VMEM((ITERS, GROUP, BLK, COLS), F32), pltpu.VMEM((ITERS, 8, BLK, COLS), F32),
             pltpu.VMEM((BLK, COLS), F32), pltpu.VMEM((BLK, COLS), F32),
             pltpu.VMEM((GROUP, 8, COLS), F32), pltpu.VMEM((GROUP, 8, COLS), F32),
+            pltpu.VMEM((8, ORDER), jnp.int32), pltpu.VMEM((DEVICES, 128), jnp.int32),
+            pltpu.VMEM((SLOTS, BLK, GROUP * BLK), F32), pltpu.VMEM((SLOTS, BLK, GROUP * BLK), F32), pltpu.VMEM((COLS, ORDER), F32),
             dma((7,)), dma((4,)), dma((JUMPS, SLOTS)), dma((JUMPS, SLOTS)), dma, dma,
             dma((ITERS,)), dma((ITERS,)), dma((ITERS,)), dma((ITERS,)), dma((ITERS, SLOTS)), dma((ITERS, SLOTS)),
-            dma((2,)), dma((2,)),
+            dma((2,)), dma((2,)), dma((SLOTS,)), dma((SLOTS,)),
         ],
         compiler_params=pltpu.CompilerParams(
             collective_id=0, has_side_effects=True, vmem_limit_bytes=63 * 1024 * 1024
         ),
         name="dual_solve",
     )(
-        applied_loads, local_inverse, schur_block, coarse_modes, coarse_rows, ids,
-        iface_rows.reshape(1, ORDER),
+        applied_loads, local_inverse, schur_block, coarse_modes, coarse_rows, mode_ids, iface_rows,
     )
-    return base + step[0:1] * direction, displaced - step[0:1] * response
+    return base + step * direction, displaced - step * response
 
 
 def solution(mesh):

time: 138 us -> 132 us (0.957)
  Pallas kernels: 131 us -> 126 us
    pallas_call x1, Pallas kernels: 131 us -> 126 us  [on_device(): pl.pallas_call(kernel, out_shape=(out, out, out, out, jax.ShapeDtypeStruc...]
    unnamed x2, local copies, waits for them, and re-layouts: 0.87 us -> 2.77 us
    reshape x2 -> x0, local copies, waits for them, and re-layouts: 1.47 us -> none  [the longest x1 0.8 us: on_device(): ids = ids.reshape(GROUP, 1, GROUP * BLK)]
where the time goes in v3:
time: 132 us
  Pallas kernels  126 us (95%)
  local copies, waits for them, and re-layouts  2.77 us (2%)
  other arithmetic  2.73 us (2%)
    pallas_call x1, Pallas kernels, on_device(): pl.pallas_call(kernel, out_shape=(out, out, out, out, jax.ShapeDtypeStruc...  126 us
    unnamed x2, local copies, waits for them, and re-layouts  2.77 us
    sub x1, other arithmetic, on_device(): return (base + step * direction, displaced - step * response)  2.73 us

profile of v3, /device:TPU:1, one launch (start us, length us, event | category | flops | bytes accessed | tf_op | source)
XLA Modules:
  0.0 132.2 jit_solution(6757585121066701785)
XLA Ops:
  0.6 1.3 copy.10.iface_in
  1.9 1.5 %copy.9.ids_in = s32[256,12]{1,0:T(8,128)} copy(s32[256,12]{0,1:T(8,128)} %param.13) | data formatting | bytes 24576 | tf_op args[5]
  3.4 126.0 %dual_solve.1 = (f32[1152,128]{1,0:T(8,128)}, f32[1152,128]{1,0:T(8,128)}, f32[1152,128]{1,0:T(8,128)}, f32[1152,128]{1,0:T(8,128)}, f32[1,128]{1,0:T(1,128)}) custom-call(f32[1152,128]{1,0:T(8,128)} %loads_hbm.1, f32[1152,1152]{1,0:T(8,128)} %inverse_hbm.1, f32[1152,1152]{1,0:T(8,128)} %schur_hbm.1, f32[12,1152]{1,0:T(8,128)} %modes_in.1, ...), custom_call_target="tpu_custom_call" | custom-call | tf_op jit(solution)/shard_map/dual_solve/pallas_call | solution.py:564
  129.4 2.7 %multiply_subtract_fusion = (f32[1152,128]{1,0:T(8,128)}, f32[1152,128]{1,0:T(8,128)}) fusion(f32[1152,128]{1,0:T(8,128)} %get-tuple-element.10, f32[1152,128]{1,0:T(8,128)} %get-tuple-element.11, f32[128]{0:T(128)} %bitcast.1, f32[1152,128]{1,0:T(8,128)} %get-tuple-element.7, f32[1152,128]{1,0:T(8,128)} %get-tuple-element.9), kind=kLoop, calls=%fused_computation | loop fusion | flops 589824 | bytes 3539456 | tf_op jit(solution)/shard_map/sub | solution.py:594
